TPU v7x, 32 devices: a whole 2x2x4 slice. The times are simulated.
32 devices in a mesh: dp: 4 (over y, x), token: 8 (over z, core).
Axes of the slice: x: 2, y: 2, z: 4, core: 2. Of those that a mesh axis runs over, the one named last changes fastest.
Arguments:
- mix_input: bfloat16 [1536, 8, 768], P('dp', 'token'), may hold values from -6 to 6
- out_grad: bfloat16 [1536, 8, 768], P('dp', 'token'), may hold values from -1.5 to 1.5
- w_up: bfloat16 [8, 768, 3072], P('token'), may hold values from -0.21875 to 0.21875
- w_down: bfloat16 [8, 3072, 768], P('token'), may hold values from -0.109375 to 0.109375
- gain_first: float32 [8, 768], P('token'), may hold values from 0.25 to 1.75
- gain_second: float32 [8, 768], P('token'), may hold values from 0.25 to 1.75
- owner_dev: int32 [8, 1536, 1], P('token', 'dp'), may hold values from 0 to 3; in each aligned block of 384 rows (0 to 383, 384 to 767, ..., all dimensions but the last counted through in order) at most 240 rows name the same one
- slot_row: int32 [8, 1536], P('token', 'dp'), may hold values from 0 to 255
Outputs:
- grad_up: float32 [8, 768, 3072], P('token', 'dp')
- grad_down: float32 [8, 3072, 768], P('token', 'dp')
- row_grad: float32 [8, 1024, 768], P('token', 'dp')
Inputs may be any that keep to these rules, and one draw needn't show every extreme that they name: `owner_dev`: in the rows of one device (aligned blocks of 384 samples of one token) no owner is named by more than 240 rows, a bound that some block reaches.
All inputs are finite; a program needn't handle non-finite values.
Results may differ from a plain program's by a relative error of at most 0.015.
Values may be sent and summed in bfloat16 or wider, within the bound.
A program may use at most 128 MiB of HBM per device.

v0:
```python
import jax
import jax.numpy as jnp
from jax import lax
from jax.sharding import PartitionSpec as P

HOT = 256


EPS = 1e-05
HALF_ROOT = 0.7071067811865476
INV_ROOT_TAU = 0.3989422804014327


def normalize(values):
    center = values - jnp.mean(values, axis=-1, keepdims=True)
    inv_scale = lax.rsqrt(jnp.mean(center * center, axis=-1, keepdims=True) + EPS)
    return (center * inv_scale, inv_scale)


def norm_back(grad_norm, normed, inv_scale):
    mean_grad = jnp.mean(grad_norm, axis=-1, keepdims=True)
    mean_proj = jnp.mean(grad_norm * normed, axis=-1, keepdims=True)
    return inv_scale * (grad_norm - mean_grad - normed * mean_proj)


def gelu_parts(pre_act):
    cumul = 0.5 * (1.0 + jax.scipy.special.erf(pre_act * HALF_ROOT))
    density = jnp.exp(-0.5 * pre_act * pre_act) * INV_ROOT_TAU
    return (pre_act * cumul, cumul + pre_act * density)


def contract_rows(left, right):
    return lax.dot_general(
        left, right, (((0,), (0,)), ((), ())), preferred_element_type=jnp.float32
    )


def contract_cols(left, right):
    return lax.dot_general(
        left, right, (((1,), (1,)), ((), ())), preferred_element_type=jnp.float32
    )


def per_device(mix_input, out_grad, w_up, w_down, gain_first, gain_second, owner_dev, slot_row):
    batch_rows = mix_input.shape[0]
    width = mix_input.shape[2]
    owners = lax.axis_size("dp")
    normed, inv_scale = normalize(mix_input[:, 0, :].astype(jnp.float32))
    hidden_in = (normed * gain_first[0]).astype(jnp.bfloat16)
    pre_act = jnp.dot(hidden_in, w_up[0], preferred_element_type=jnp.float32)
    act_value, act_slope = gelu_parts(pre_act)
    active = act_value.astype(jnp.bfloat16)
    outer_sum = jnp.dot(active, w_down[0], preferred_element_type=jnp.float32) + hidden_in.astype(
        jnp.float32
    )
    normed_out, inv_out = normalize(outer_sum)
    grad_wide = norm_back(
        out_grad[:, 0, :].astype(jnp.float32) * gain_second[0], normed_out, inv_out
    )
    grad_mid = grad_wide.astype(jnp.bfloat16)
    grad_act = contract_cols(grad_mid, w_down[0])
    grad_pre = (grad_act * act_slope).astype(jnp.bfloat16)
    up_whole = contract_rows(hidden_in, grad_pre)
    down_whole = contract_rows(active, grad_mid)
    grad_up, grad_down = (
        lax.psum_scatter(
            up_whole.astype(jnp.bfloat16), "dp", scatter_dimension=0, tiled=True
        ).astype(jnp.float32),
        lax.psum_scatter(
            down_whole.astype(jnp.bfloat16), "dp", scatter_dimension=0, tiled=True
        ).astype(jnp.float32),
    )
    grad_hidden = contract_cols(grad_pre, w_up[0]) + grad_wide
    grad_sum = norm_back(grad_hidden * gain_first[0], normed, inv_scale).astype(jnp.bfloat16)
    pieces = lax.axis_size("token")
    swapped = lax.all_to_all(
        grad_sum.reshape(batch_rows, pieces, width // pieces),
        "token",
        split_axis=1,
        concat_axis=1,
        tiled=True,
    )
    embed_grad = (
        grad_sum.astype(jnp.float32) + swapped.reshape(batch_rows, width).astype(jnp.float32)
    ).astype(jnp.bfloat16)
    owner_ids = owner_dev[0, :, 0]
    slot_ids = slot_row[0]
    capacity = max(2, 8 * (5 * batch_rows // (16 * owners)))
    owner_hot = (
        owner_ids[:, None] == lax.broadcasted_iota(jnp.int32, (batch_rows, owners), 1)
    ).astype(jnp.int32)
    rank_within = jnp.sum((jnp.cumsum(owner_hot, axis=0) - 1) * owner_hot, axis=1)
    place = owner_ids * capacity + rank_within
    dispatch_mask = (
        lax.broadcasted_iota(jnp.int32, (owners * capacity, batch_rows), 0) == place[None, :]
    )
    send_grad = jnp.dot(
        dispatch_mask.astype(jnp.bfloat16), embed_grad, preferred_element_type=jnp.float32
    )
    send_grad = send_grad.astype(jnp.bfloat16).reshape(owners, capacity, width)
    send_slot = jnp.sum(dispatch_mask.astype(jnp.int32) * (slot_ids + 1)[None, :], axis=1) - 1
    send_slot = send_slot.astype(jnp.float32).astype(jnp.bfloat16).reshape(owners, capacity)
    recv_grad, recv_slot = (
        lax.all_to_all(send_grad, "dp", split_axis=0, concat_axis=0, tiled=True),
        lax.all_to_all(send_slot, "dp", split_axis=0, concat_axis=0, tiled=True),
    )
    slot_values = recv_slot.reshape(1, owners * capacity).astype(jnp.float32)
    gather_hot = (
        lax.broadcasted_iota(jnp.int32, (HOT, owners * capacity), 0).astype(jnp.float32)
        == slot_values
    ).astype(jnp.bfloat16)
    row_grad = jnp.dot(
        gather_hot, recv_grad.reshape(owners * capacity, width), preferred_element_type=jnp.float32
    )
    return (grad_up[None], grad_down[None], row_grad[None])


def solution(mesh):
    placed = (
        P("dp", "token", None),
        P("dp", "token", None),
        P("token", None, None),
        P("token", None, None),
        P("token", None),
        P("token", None),
        P("token", "dp", None),
        P("token", "dp"),
    )
    return jax.shard_map(
        per_device,
        mesh=mesh,
        in_specs=placed,
        out_specs=(P("token", "dp", None), P("token", "dp", None), P("token", "dp", None)),
        check_vma=False,
    )
```

profile of v0, /device:TPU:0, one launch (start us, length us, event | category | flops | bytes accessed | tf_op | source)
XLA Modules:
  0.0 167.2 jit_solution(3373217656529832667)
XLA Ops:
  7.2 0.0 copy-start
  7.2 0.0 copy-start.2
  7.2 0.0 copy-start.3
  7.2 0.0 reduce-scatter.5.cloned.1.call-start
  7.2 1.3 convert_reduce_fusion
  8.5 1.4 fusion.36
  9.9 0.0 copy-done.2
  9.9 0.0 copy-done.3
  10.0 0.0 copy-done
  10.0 6.4 %multiply_convert_fusion = (bf16[384,3072]{1,0:T(8,128)(2,1)S(1)}, f32[384,3072]{1,0:T(8,128)}) fusion(bf16[1,768,3072]{2,1,0:T(8,128)(2,1)} %param.10, bf16[384,1,768]{2,0,1:T(8,128)(2,1)S(1)} %copy-done, f32[768]{0:T(1024)S(1)} %reduce.1, f32[384]{0:T(512)S(1)} %add_rsqrt_fusion.1, f32[384]{0:T(512)S(1)} %broadcast_multiply_fusion.5), kind=kOutput, calls=%fused_computation.17 | convolution fusion | flops 1819312128 | bytes 12392448 | tf_op jit(solution)/shard_map/dot_general | solution.py:50
  16.4 4.4 %fusion.64 = (f32[384]{0:T(512)S(1)}, f32[384,768]{1,0:T(8,128)S(1)}) fusion(f32[768]{0:T(1024)S(1)} %reduce.1, f32[384]{0:T(512)S(1)} %add_rsqrt_fusion.1, f32[384]{0:T(512)S(1)} %broadcast_multiply_fusion.5, bf16[384,1,768]{2,0,1:T(8,128)(2,1)S(1)} %copy-done, bf16[384,3072]{1,0:T(8,128)(2,1)S(1)} %get-tuple-element.7, bf16[1,3072,768]{2,1,0:T(8,128)(2,1)} %param.11), kind=kOutput, calls=%fused_computation.88 | convolution fusion | flops 1814298240 | bytes 8855040 | tf_op jit(solution)/shard_map/dot_general | solution.py:53
  20.8 0.0 copy-start.1
  20.8 0.3 multiply_reduce_fusion
  21.1 0.8 copy-done.1
  21.9 0.4 fusion.42
  22.3 4.7 %convolution_convert_fusion = bf16[3072,768]{1,0:T(8,128)(2,1)} fusion(bf16[384,3072]{1,0:T(8,128)(2,1)S(1)} %get-tuple-element.7, f32[384,768]{1,0:T(8,128)S(1)} %get-tuple-element.10, bf16[384,1,768]{2,0,1:T(8,128)(2,1)S(1)} %copy-done.1, f32[384]{0:T(512)S(1)} %get-tuple-element.12, f32[384]{0:T(512)S(1)} %get-tuple-element.13, f32[768]{0:T(1024)S(1)} %reduce.2, ...), kind=kOutput, calls=%fused_computation.1 | convolution fusion | flops 1816952832 | bytes 8856576 | tf_op jit(solution)/shard_map/dot_general | solution.py:33
  27.0 0.0 reduce-scatter.5.cloned.1.call-update
  27.0 0.0 reduce-scatter.3.cloned.1.call-start
  27.0 6.8 %fusion.5 = bf16[384,3072]{1,0:T(8,128)(2,1)S(1)} fusion(f32[384,3072]{1,0:T(8,128)} %get-tuple-element.8, bf16[1,3072,768]{2,1,0:T(8,128)(2,1)} %param.11, f32[384,768]{1,0:T(8,128)S(1)} %get-tuple-element.10, bf16[384,1,768]{2,0,1:T(8,128)(2,1)S(1)} %copy-done.1, f32[384]{0:T(512)S(1)} %get-tuple-element.12, f32[384]{0:T(512)S(1)} %get-tuple-element.13, ...), kind=kOutput, calls=%fused_computation.8 | convolution fusion | flops 1826390016 | bytes 13575168 | tf_op jit(solution)/shard_map/dot_general | solution.py:39
  33.9 0.0 copy-start.6
  33.9 1.4 copy-done.6
  35.3 4.7 %convolution_convert_fusion.1 = bf16[768,3072]{1,0:T(8,128)(2,1)} fusion(bf16[384,3072]{1,0:T(8,128)(2,1)S(1)} %fusion.5, bf16[384,1,768]{2,0,1:T(8,128)(2,1)S(1)} %copy-done, f32[768]{0:T(1024)S(1)} %reduce.1, f32[384]{0:T(512)S(1)} %add_rsqrt_fusion.1, f32[384]{0:T(512)S(1)} %broadcast_multiply_fusion.5), kind=kOutput, calls=%fused_computation.2 | convolution fusion | flops 1815773184 | bytes 7673856 | tf_op jit(solution)/shard_map/dot_general | solution.py:33
  40.0 0.0 reduce-scatter.3.cloned.1.call-update
  40.0 5.5 %fusion.63 = (f32[384]{0:T(512)S(1)}, f32[384]{0:T(512)S(1)}, f32[384,768]{1,0:T(8,128)S(1)}) fusion(f32[384]{0:T(512)S(1)} %add_rsqrt_fusion.1, f32[384]{0:T(512)S(1)} %broadcast_multiply_fusion.5, bf16[384,1,768]{2,0,1:T(8,128)(2,1)S(1)} %copy-done, f32[768]{0:T(1024)S(1)} %reduce.1, f32[384]{0:T(512)S(1)} %get-tuple-element.12, ...), kind=kOutput, calls=%fused_computation.87 | convolution fusion | flops 1816657152 | bytes 10635264 | tf_op jit(solution)/shard_map/dot_general | solution.py:39
  45.5 0.4 fusion.35
  45.9 0.0 copy-start.5
  45.9 0.0 copy-start.4
  45.9 1.1 copy.17
  47.0 6.6 %all-to-all-start.1 = ((bf16[384,8,96]{0,2,1:T(8,128)(2,1)}), bf16[384,8,96]{0,2,1:T(8,128)(2,1)S(1)}, u32[]{:S(2)}, u32[]{:S(2)}) async-start(bf16[384,8,96]{0,2,1:T(8,128)(2,1)} %bitcast.8), calls=%async_computation.3 | async-start | bytes 1179648 | tf_op jit(solution)/shard_map/all_to_all | solution.py:76
  53.6 0.0 copy-done.5
  53.7 1.2 reduce-window.6
  54.9 0.2 slice_reduce_fusion
  55.1 0.2 reduce-window.9
  55.3 0.0 copy-done.4
  55.3 0.1 add_bitcast_fusion
  55.4 0.2 select_reduce_fusion
  55.7 0.7 convert_element_type.137
  56.4 14.0 %all-to-all-done.1 = bf16[384,8,96]{0,2,1:T(8,128)(2,1)S(1)} async-done(((bf16[384,8,96]{0,2,1:T(8,128)(2,1)}), bf16[384,8,96]{0,2,1:T(8,128)(2,1)S(1)}, u32[]{:S(2)}, u32[]{:S(2)}) %all-to-all-start.1) | async-done | bytes 589856 | tf_op jit(solution)/shard_map/all_to_all | solution.py:76
  70.4 3.7 %all-to-all-start = ((bf16[4,1,240]{2,1,0:T(2,128)(2,1)}), bf16[4,1,240]{2,1,0:T(2,128)(2,1)S(1)}, u32[]{:S(2)}, u32[]{:S(2)}) async-start(bf16[4,1,240]{2,1,0:T(2,128)(2,1)} %convert_element_type.137), calls=%async_computation.2 | async-start | bytes 8192 | tf_op jit(solution)/shard_map/all_to_all | solution.py:105
  74.1 0.1 bitcast_convert_fusion.2
  74.2 0.4 copy.18
  74.6 2.1 %convolution_convert_fusion.2 = bf16[960,768]{1,0:T(8,128)(2,1)} fusion(s32[384]{0:T(512)S(1)} %multiply_add_fusion, f32[384,768]{1,0:T(8,128)S(1)} %copy.18, bf16[384,768]{1,0:T(8,128)(2,1)S(1)} %fusion.35), kind=kOutput, calls=%fused_computation.22 | convolution fusion | flops 568221696 | bytes 3245568 | tf_op jit(solution)/shard_map/dot_general | solution.py:97
  76.7 2.2 %all-to-all-done = bf16[4,1,240]{2,1,0:T(2,128)(2,1)S(1)} async-done(((bf16[4,1,240]{2,1,0:T(2,128)(2,1)}), bf16[4,1,240]{2,1,0:T(2,128)(2,1)S(1)}, u32[]{:S(2)}, u32[]{:S(2)}) %all-to-all-start) | async-done | bytes 1952 | tf_op jit(solution)/shard_map/all_to_all | solution.py:105
  78.9 3.6 %all-to-all-start.2 = ((bf16[4,240,768]{2,1,0:T(8,128)(2,1)}), bf16[4,240,768]{2,1,0:T(8,128)(2,1)S(1)}, u32[]{:S(2)}, u32[]{:S(2)}) async-start(bf16[4,240,768]{2,1,0:T(8,128)(2,1)} %bitcast.10), calls=%async_computation.4 | async-start | bytes 2949120 | tf_op jit(solution)/shard_map/all_to_all | solution.py:104
  82.5 0.1 reshape.147
  82.6 18.5 %all-to-all-done.2 = bf16[4,240,768]{2,1,0:T(8,128)(2,1)S(1)} async-done(((bf16[4,240,768]{2,1,0:T(8,128)(2,1)}), bf16[4,240,768]{2,1,0:T(8,128)(2,1)S(1)}, u32[]{:S(2)}, u32[]{:S(2)}) %all-to-all-start.2) | async-done | bytes 1474592 | tf_op jit(solution)/shard_map/all_to_all | solution.py:104
  101.1 1.5 convolution_bitcast_fusion
  102.6 0.0 reduce-scatter.5.cloned.1.call-done
  102.6 2.8 %bitcast_convert_fusion = f32[1,768,768]{2,1,0:T(8,128)} fusion(bf16[768,768]{1,0:T(8,128)(2,1)} %reduce-scatter.5.cloned.1.call-done), kind=kLoop, calls=%fused_computation.44 | loop fusion | flops 589824 | bytes 3538944 | tf_op jit(solution)/shard_map/broadcast_in_dim | solution.py:115
  105.5 52.0 %reduce-scatter.3.cloned.1.call-done = bf16[192,3072]{1,0:T(8,128)(2,1)} async-done(((bf16[768,3072]{1,0:T(8,128)(2,1)}), bf16[192,3072]{1,0:T(8,128)(2,1)}) %reduce-scatter.3.cloned.1.call-update) | async-done | bytes 1179664 | tf_op jit(solution)/shard_map/reduce_scatter | solution.py:66
  157.5 2.9 %bitcast_convert_fusion.1 = f32[1,192,3072]{2,1,0:T(8,128)} fusion(bf16[192,3072]{1,0:T(8,128)(2,1)} %reduce-scatter.3.cloned.1.call-done), kind=kLoop, calls=%fused_computation.45 | loop fusion | flops 589824 | bytes 3538944 | tf_op jit(solution)/shard_map/broadcast_in_dim | solution.py:115
  (17 shorter events, 0.2 us)
Async XLA Ops:
  7.2 2.8 %copy-start = (bf16[384,1,768]{2,0,1:T(8,128)(2,1)S(1)}, bf16[384,1,768]{2,0,1:T(8,128)(2,1)}, u32[]{:S(2)}) copy-start(bf16[384,1,768]{2,0,1:T(8,128)(2,1)} %param.8) | copy-start | bytes 1769476
  7.2 2.7 %copy-start.2 = (f32[1,768]{1,0:T(1,128)S(1)}, f32[1,768]{1,0:T(1,128)}, u32[]{:S(2)}) copy-start(f32[1,768]{1,0:T(1,128)} %param.12) | copy-start | bytes 9220
  7.2 2.7 %copy-start.3 = (f32[1,768]{1,0:T(1,128)S(1)}, f32[1,768]{1,0:T(1,128)}, u32[]{:S(2)}) copy-start(f32[1,768]{1,0:T(1,128)} %param.13) | copy-start | bytes 9220
  7.2 95.4 %reduce-scatter.5.cloned.1.call-start = ((), (), s32[]{:S(2)}) async-start(), calls=%async_computation.6 | async-start | bytes 5898240 | tf_op jit(solution)/shard_map/reduce_scatter | solution.py:69
  20.8 1.1 copy-start.1
  27.0 130.5 %reduce-scatter.3.cloned.1.call-start = ((), (), s32[]{:S(2)}) async-start(), calls=%async_computation.5 | async-start | bytes 5898240 | tf_op jit(solution)/shard_map/reduce_scatter | solution.py:66
  33.9 1.4 copy-start.6
  45.9 7.7 %copy-start.5 = (s32[1,384,1]{1,2,0:T(1,128)S(1)}, s32[1,384,1]{1,2,0:T(1,128)}, u32[]{:S(2)}) copy-start(s32[1,384,1]{1,2,0:T(1,128)} %param.14) | copy-start | bytes 4612
  45.9 9.4 %copy-start.4 = (s32[1,384]{1,0:T(1,128)S(1)}, s32[1,384]{1,0:T(1,128)}, u32[]{:S(2)}) copy-start(s32[1,384]{1,0:T(1,128)} %param.15) | copy-start | bytes 4612
  47.0 23.4 %all-to-all-start.1 = ((bf16[384,8,96]{0,2,1:T(8,128)(2,1)}), bf16[384,8,96]{0,2,1:T(8,128)(2,1)S(1)}, u32[]{:S(2)}, u32[]{:S(2)}) async-start(bf16[384,8,96]{0,2,1:T(8,128)(2,1)} %bitcast.8), calls=%async_computation.3 | async-start | bytes 1179648 | tf_op jit(solution)/shard_map/all_to_all | solution.py:76
  70.4 8.5 %all-to-all-start = ((bf16[4,1,240]{2,1,0:T(2,128)(2,1)}), bf16[4,1,240]{2,1,0:T(2,128)(2,1)S(1)}, u32[]{:S(2)}, u32[]{:S(2)}) async-start(bf16[4,1,240]{2,1,0:T(2,128)(2,1)} %convert_element_type.137), calls=%async_computation.2 | async-start | bytes 8192 | tf_op jit(solution)/shard_map/all_to_all | solution.py:105
  78.9 22.2 %all-to-all-start.2 = ((bf16[4,240,768]{2,1,0:T(8,128)(2,1)}), bf16[4,240,768]{2,1,0:T(8,128)(2,1)S(1)}, u32[]{:S(2)}, u32[]{:S(2)}) async-start(bf16[4,240,768]{2,1,0:T(8,128)(2,1)} %bitcast.10), calls=%async_computation.4 | async-start | bytes 2949120 | tf_op jit(solution)/shard_map/all_to_all | solution.py:104
Sparse Core Ops, SparseCore 0:
  27.1 68.5 reduce-scatter.4
  98.7 58.7 reduce-scatter.2
where the time goes:
time: 168 us; the launch traced here: 167 us
  waiting for transfers between devices  86.8 us (52%)
  matrix products  36.1 us (21%)
  between operations  14.2 us (8%)
  starting transfers between devices  14 us (8%)
  other arithmetic  11.5 us (7%)
  local copies, waits for them, and re-layouts  4.61 us (3%)
    reduce_scatter x1, waiting for transfers between devices, per_device(): lax.psum_scatter(up_whole.astype(jnp.bfloat16), 'dp', scatter_dimension=0...  52 us
    all_to_all x1, waiting for transfers between devices, per_device(): lax.all_to_all(send_grad, 'dp', split_axis=0, concat_axis=0, tiled=True)  18.5 us
    all_to_all x1, waiting for transfers between devices, per_device(): lax.all_to_all(grad_sum.reshape(batch_rows, pieces, width // pieces), 'to...  14 us
    dot_general x2, matrix products, contract_cols(): lax.dot_general(left, right, (((1,), (1,)), ((), ())), preferred_element_...  12.3 us
    dot_general x2, matrix products, contract_rows(): lax.dot_general(left, right, (((0,), (0,)), ((), ())), preferred_element_...  9.4 us
    all_to_all x1, starting transfers between devices, per_device(): lax.all_to_all(grad_sum.reshape(batch_rows, pieces, width // pieces), 'to...  6.64 us
    dot_general x1, matrix products, per_device(): pre_act = jnp.dot(hidden_in, w_up[0], preferred_element_type=jnp.float32)  6.38 us
    broadcast_in_dim x2, other arithmetic, per_device(): return (grad_up[None], grad_down[None], row_grad[None])  5.78 us
  transfers between devices with their start and end apart: 5, of which 4 were waited for; matrix products, arithmetic and copies ran while one was open for 17% of the time, Pallas kernels for 0%

commit v1 on v0

--- a/solution.py
+++ b/solution.py
@@ -1,6 +1,10 @@
+import functools
+
 import jax
 import jax.numpy as jnp
 from jax import lax
+from jax.experimental import pallas as pl
+from jax.experimental.pallas import tpu as pltpu
 from jax.sharding import PartitionSpec as P
 
 HOT = 256
@@ -115,6 +119,249 @@
     return (grad_up[None], grad_down[None], row_grad[None])
 
 
+TILE = 512
+VMEM_BYTES = 60 * 1024 * 1024
+
+
+def dot_rows(left, right):
+    return lax.dot_general(
+        left, right, (((0,), (0,)), ((), ())), preferred_element_type=jnp.float32
+    )
+
+
+def forward_kernel(h_ref, up_ref, down_ref, grad_ref, gain_ref, act_ref, slope_ref, wide_ref, mid_ref, acc):
+    step = pl.program_id(0)
+    pre = jnp.dot(h_ref[...], up_ref[...], preferred_element_type=jnp.float32)
+    value, slope = gelu_parts(pre)
+    act = value.astype(jnp.bfloat16)
+    act_ref[...] = act
+    slope_ref[...] = slope.astype(jnp.bfloat16)
+    part = jnp.dot(act, down_ref[...], preferred_element_type=jnp.float32)
+
+    @pl.when(step == 0)
+    def _():
+        acc[...] = part + h_ref[...].astype(jnp.float32)
+
+    @pl.when(step > 0)
+    def _():
+        acc[...] += part
+
+    @pl.when(step == pl.num_programs(0) - 1)
+    def _():
+        normed, inv = normalize(acc[...])
+        wide = norm_back(grad_ref[...].astype(jnp.float32) * gain_ref[...], normed, inv)
+        wide_ref[...] = wide
+        mid_ref[...] = wide.astype(jnp.bfloat16)
+
+
+def backward_kernel(mid_ref, down_ref, up_ref, slope_ref, wide_ref, mix_ref, gain_ref, pre_ref, sum_ref, acc):
+    step = pl.program_id(0)
+    grad_act = contract_cols(mid_ref[...], down_ref[...])
+    grad_pre = (grad_act * slope_ref[...].astype(jnp.float32)).astype(jnp.bfloat16)
+    pre_ref[...] = grad_pre
+    part = contract_cols(grad_pre, up_ref[...])
+
+    @pl.when(step == 0)
+    def _():
+        acc[...] = part + wide_ref[...]
+
+    @pl.when(step > 0)
+    def _():
+        acc[...] += part
+
+    @pl.when(step == pl.num_programs(0) - 1)
+    def _():
+        normed, inv = normalize(mix_ref[...].astype(jnp.float32))
+        grad_sum = norm_back(acc[...] * gain_ref[...], normed, inv)
+        sum_ref[...] = grad_sum.T.astype(jnp.bfloat16)
+
+
+def others_kernel(own_tiles, me_ref, *refs):
+    h_refs = refs[: len(refs) - 3]
+    up_ref, slope_ref, act_ref = refs[len(refs) - 3 :]
+    for g, h_ref in enumerate(h_refs):
+        pre = jnp.dot(h_ref[...], up_ref[...], preferred_element_type=jnp.float32)
+        value, slope = gelu_parts(pre)
+        slope_ref[g] = slope.astype(jnp.bfloat16)
+
+        @pl.when(pl.program_id(0) < own_tiles)
+        def _():
+            act_ref[g] = value.astype(jnp.bfloat16)
+
+
+def up_kernel(groups, *refs):
+    mid_refs = refs[: groups - 1]
+    hsel_ref, down_ref, slope_ref, own_ref, up_ref = refs[groups - 1 :]
+    rows = own_ref.shape[0]
+    total = jnp.dot(hsel_ref[:, :rows], own_ref[...], preferred_element_type=jnp.float32)
+    for g in range(groups - 1):
+        grad_act = contract_cols(mid_refs[g][...], down_ref[...])
+        grad_pre = (grad_act * slope_ref[g].astype(jnp.float32)).astype(jnp.bfloat16)
+        total += jnp.dot(
+            hsel_ref[:, (g + 1) * rows : (g + 2) * rows], grad_pre, preferred_element_type=jnp.float32
+        )
+    up_ref[...] = total
+
+
+def down_kernel(me_ref, own_ref, act_ref, *refs):
+    mid_refs, out_ref = refs[:-1], refs[-1]
+    total = dot_rows(own_ref[...], mid_refs[0][...])
+    for g in range(len(mid_refs) - 1):
+        total += dot_rows(act_ref[g], mid_refs[g + 1][...])
+    out_ref[...] = total
+
+
+def params():
+    return pltpu.CompilerParams(vmem_limit_bytes=VMEM_BYTES)
+
+
+def whole(*shape):
+    return pl.BlockSpec(shape, lambda f, *_: (0,) * len(shape))
+
+
+def cost(flops, nbytes):
+    return pl.CostEstimate(flops=int(flops), bytes_accessed=int(nbytes), transcendentals=0)
+
+
+def gather_groups(value, groups):
+    return [
+        lax.ppermute(value, "dp", [(i, i ^ k) for i in range(groups)]) for k in range(1, groups)
+    ]
+
+
+def small_group(mix_input, out_grad, w_up, w_down, gain_first, gain_second, owner_dev, slot_row):
+    rows = mix_input.shape[0]
+    width = mix_input.shape[2]
+    hidden = w_up.shape[2]
+    groups = lax.axis_size("dp")
+    pieces = lax.axis_size("token")
+    me = lax.axis_index("dp")
+    me_arr = me.astype(jnp.int32).reshape(1)
+    up_mat, down_mat = w_up[0], w_down[0]
+    mix = mix_input[:, 0, :]
+    grad = out_grad[:, 0, :]
+    normed, _ = normalize(mix.astype(jnp.float32))
+    hidden_in = (normed * gain_first[0]).astype(jnp.bfloat16)
+    others_h = gather_groups(hidden_in, groups)
+    steps = hidden // TILE
+    bf, f32 = jnp.bfloat16, jnp.float32
+    unit = 2 * rows * width * hidden
+    wbytes = 2 * width * hidden
+    up_spec = pl.BlockSpec((width, TILE), lambda f, *_: (0, f))
+    down_spec = pl.BlockSpec((TILE, width), lambda f, *_: (f, 0))
+    col_spec = pl.BlockSpec((rows, TILE), lambda f, *_: (0, f))
+    active, slope, wide, mid = pl.pallas_call(
+        forward_kernel,
+        grid=(steps,),
+        in_specs=[whole(rows, width), up_spec, down_spec, whole(rows, width), whole(1, width)],
+        out_specs=[col_spec, col_spec, whole(rows, width), whole(rows, width)],
+        out_shape=[
+            jax.ShapeDtypeStruct((rows, hidden), bf),
+            jax.ShapeDtypeStruct((rows, hidden), bf),
+            jax.ShapeDtypeStruct((rows, width), f32),
+            jax.ShapeDtypeStruct((rows, width), bf),
+        ],
+        scratch_shapes=[pltpu.VMEM((rows, width), f32)],
+        compiler_params=params(),
+        cost_estimate=cost(2 * unit, 3 * wbytes),
+        name="forward",
+    )(hidden_in, up_mat, down_mat, grad, gain_second)
+    others_mid = gather_groups(mid, groups)
+    grad_pre, sum_t = pl.pallas_call(
+        backward_kernel,
+        grid=(steps,),
+        in_specs=[
+            whole(rows, width), down_spec, up_spec, col_spec,
+            whole(rows, width), whole(rows, width), whole(1, width),
+        ],
+        out_specs=[col_spec, whole(width, rows)],
+        out_shape=[
+            jax.ShapeDtypeStruct((rows, hidden), bf),
+            jax.ShapeDtypeStruct((width, rows), bf),
+        ],
+        scratch_shapes=[pltpu.VMEM((rows, width), f32)],
+        compiler_params=params(),
+        cost_estimate=cost(2 * unit, 3 * wbytes),
+        name="backward",
+    )(mid, down_mat, up_mat, slope, wide, mix, gain_first)
+
+    swapped = lax.all_to_all(
+        sum_t.reshape(pieces, width // pieces, rows), "token", split_axis=0, concat_axis=0, tiled=True
+    ).reshape(width, rows)
+
+    own_cols = hidden // groups
+    tile_a = min(TILE, own_cols // 2)
+    own_tiles = own_cols // tile_a
+    steps_a = hidden // tile_a
+    o_slope, o_act = pl.pallas_call(
+        functools.partial(others_kernel, own_tiles),
+        grid_spec=pltpu.PrefetchScalarGridSpec(
+            num_scalar_prefetch=1,
+            grid=(steps_a,),
+            in_specs=[whole(rows, width)] * (groups - 1)
+            + [pl.BlockSpec((width, tile_a), lambda f, m: (0, lax.rem(f + m[0] * own_tiles, steps_a)))],
+            out_specs=[
+                pl.BlockSpec((groups - 1, rows, tile_a), lambda f, m: (0, 0, lax.rem(f + m[0] * own_tiles, steps_a))),
+                pl.BlockSpec((groups - 1, rows, tile_a), lambda f, m: (0, 0, jnp.minimum(f, own_tiles - 1))),
+            ],
+        ),
+        out_shape=[
+            jax.ShapeDtypeStruct((groups - 1, rows, hidden), bf),
+            jax.ShapeDtypeStruct((groups - 1, rows, own_cols), bf),
+        ],
+        compiler_params=params(),
+        cost_estimate=cost((groups - 1) * unit, 3 * wbytes),
+        name="others",
+    )(me_arr, *others_h, up_mat)
+
+    out_rows = width // groups
+    hsel = jnp.concatenate(
+        [lax.dynamic_slice(h, (0, me * out_rows), (rows, out_rows)).T for h in [hidden_in] + others_h], axis=1
+    )
+    grad_up = pl.pallas_call(
+        functools.partial(up_kernel, groups),
+        grid=(steps,),
+        in_specs=[whole(rows, width)] * (groups - 1)
+        + [
+            whole(out_rows, groups * rows), down_spec,
+            pl.BlockSpec((groups - 1, rows, TILE), lambda f: (0, 0, f)), col_spec,
+        ],
+        out_specs=pl.BlockSpec((out_rows, TILE), lambda f: (0, f)),
+        out_shape=jax.ShapeDtypeStruct((out_rows, hidden), f32),
+        compiler_params=params(),
+        cost_estimate=cost(groups * unit, 5 * wbytes),
+        name="upgrad",
+    )(*others_mid, hsel, down_mat, o_slope, grad_pre)
+
+    part = own_cols // 3 if own_cols % 384 == 0 else own_cols
+    parts = own_cols // part
+    grad_down = pl.pallas_call(
+        down_kernel,
+        grid_spec=pltpu.PrefetchScalarGridSpec(
+            num_scalar_prefetch=1,
+            grid=(parts,),
+            in_specs=[
+                pl.BlockSpec((rows, part), lambda f, m: (0, f + m[0] * parts)),
+                pl.BlockSpec((groups - 1, rows, part), lambda f, m: (0, 0, f)),
+            ]
+            + [whole(rows, width)] * groups,
+            out_specs=pl.BlockSpec((part, width), lambda f, m: (f, 0)),
+        ),
+        out_shape=jax.ShapeDtypeStruct((own_cols, width), f32),
+        compiler_params=params(),
+        cost_estimate=cost(unit, 2 * wbytes),
+        name="downgrad",
+    )(me_arr, active, o_act, mid, *others_mid)
+
+    embed_t = (sum_t.astype(f32) + swapped.astype(f32)).astype(bf)
+    target = owner_dev[0, :, 0] * HOT + slot_row[0]
+    hot = (lax.broadcasted_iota(jnp.int32, (groups * HOT, rows), 0) == target[None, :]).astype(bf)
+    partial_rows = contract_cols(hot, embed_t).astype(bf).reshape(groups, HOT, width)
+    received = lax.all_to_all(partial_rows, "dp", split_axis=0, concat_axis=0, tiled=True)
+    row_grad = jnp.sum(received.astype(f32), axis=0)
+    return (grad_up[None], grad_down[None], row_grad[None])
+
+
 def solution(mesh):
     placed = (
         P("dp", "token", None),
@@ -127,7 +374,7 @@
         P("token", "dp"),
     )
     return jax.shard_map(
-        per_device,
+        small_group if mesh.shape["dp"] <= 4 else per_device,
         mesh=mesh,
         in_specs=placed,
         out_specs=(P("token", "dp", None), P("token", "dp", None), P("token", "dp", None)),

time: 168 us -> 95.6 us (0.57)
  waiting for transfers between devices: 86.8 us -> 0.02 us
  Pallas kernels: 0 us -> 63.8 us
  matrix products: 36.1 us -> 3.3 us
  between operations: 14.2 us -> 0.76 us
  other arithmetic: 11.5 us -> 2.56 us
  starting transfers between devices: 14 us -> 17.4 us
  local copies, waits for them, and re-layouts: 4.61 us -> 7.11 us
    pallas_call x0 -> x5, Pallas kernels: none -> 63.8 us  [the longest x1 18.4 us: small_group(): pl.pallas_call(functools.partial(others_kernel, own_tiles), grid_spec=plt...]
    reduce_scatter x2 -> x0, waiting for transfers between devices: 52 us -> none  [the longest x1 52 us: per_device(): lax.psum_scatter(up_whole.astype(jnp.bfloat16), 'dp', scatter_dimension=0...]
    all_to_all x3 -> x2, waiting for transfers between devices: 34.7 us -> 0.01 us  [the longest x1 0.01 us: small_group(): lax.all_to_all(sum_t.reshape(pieces, width // pieces, rows), 'token', spl...]
    dot_general x6 -> x0, matrix products: 23.8 us -> none  [the longest x2 9.4 us: contract_rows(): lax.dot_general(left, right, (((0,), (0,)), ((), ())), preferred_element_...]
    dot_general x2 -> x1, matrix products: 12.3 us -> 3.3 us  [contract_cols(): lax.dot_general(left, right, (((1,), (1,)), ((), ())), preferred_element_...]
    ppermute x0 -> x6, starting transfers between devices: none -> 8.25 us  [gather_groups(): lax.ppermute(value, 'dp', [(i, i ^ k) for i in range(groups)])]
    broadcast_in_dim x2 -> x0, other arithmetic: 5.78 us -> none  [per_device(): return (grad_up[None], grad_down[None], row_grad[None])]
    all_to_all x3 -> x2, starting transfers between devices: 13.9 us -> 9.12 us  [the longest x1 5.42 us: small_group(): lax.all_to_all(sum_t.reshape(pieces, width // pieces, rows), 'token', spl...]
  transfers between devices with their start and end apart: 5 -> 8, of which waited for: 4 -> 0; matrix products, arithmetic and copies ran while one was open for 17% -> 10% of each run, Pallas kernels for 0% -> 67%
where the time goes in v1:
time: 95.6 us; the launch traced here: 95 us
  Pallas kernels  63.8 us (67%)
  starting transfers between devices  17.4 us (18%)
  local copies, waits for them, and re-layouts  7.11 us (7%)
  matrix products  3.3 us (3%)
  other arithmetic  2.56 us (3%)
    pallas_call x1, Pallas kernels, small_group(): pl.pallas_call(functools.partial(others_kernel, own_tiles), grid_spec=plt...  18.4 us
    pallas_call x1, Pallas kernels, small_group(): pl.pallas_call(functools.partial(up_kernel, groups), grid=(steps,), in_sp...  15 us
    pallas_call x1, Pallas kernels, small_group(): pl.pallas_call(backward_kernel, grid=(steps,), in_specs=[whole(rows, widt...  12.1 us
    pallas_call x1, Pallas kernels, small_group(): pl.pallas_call(forward_kernel, grid=(steps,), in_specs=[whole(rows, width...  12 us
    ppermute x6, starting transfers between devices, gather_groups(): lax.ppermute(value, 'dp', [(i, i ^ k) for i in range(groups)])  8.25 us
    pallas_call x1, Pallas kernels, small_group(): pl.pallas_call(down_kernel, grid_spec=pltpu.PrefetchScalarGridSpec(num_sc...  6.36 us
    all_to_all x1, starting transfers between devices, small_group(): lax.all_to_all(sum_t.reshape(pieces, width // pieces, rows), 'token', spl...  5.42 us
    all_to_all x1, starting transfers between devices, small_group(): lax.all_to_all(partial_rows, 'dp', split_axis=0, concat_axis=0, tiled=True)  3.7 us
  transfers between devices with their start and end apart: 8, of which 0 were waited for; matrix products, arithmetic and copies ran while one was open for 10% of the time, Pallas kernels for 67%

profile of v1, /device:TPU:0, one launch (start us, length us, event | category | flops | bytes accessed | tf_op | source)
XLA Modules:
  0.0 95.0 jit_solution(17202405226885935154)
XLA Ops:
  0.6 0.0 copy-start.4
  0.6 1.4 %copy.11 = bf16[384,1,768]{0,2,1:T(8,128)(2,1)S(1)} copy(bf16[384,1,768]{2,0,1:T(8,128)(2,1)} %param.8) | data formatting | bytes 1179648 | tf_op args[0]
  2.0 0.1 convert_reduce_fusion.1
  2.2 0.2 fusion.2
  2.4 0.0 copy-done.4
  2.4 0.2 fusion.4
  2.6 4.0 %collective-permute-start.5 = (bf16[384,768]{0,1:T(8,128)(2,1)S(1)}, bf16[384,768]{0,1:T(8,128)(2,1)S(1)}, u32[]{:S(2)}, u32[]{:S(2)}) collective-permute-start(bf16[384,768]{0,1:T(8,128)(2,1)S(1)} %fusion.4), channel_id=1, source_target_pairs={{0,24},{8,16},{16,8},{24,0},{1,25},{9,17},{17,9},{25,1},{2,26},{10... | collective-permute-start | bytes 1769480 | tf_op jit(solution)/shard_map/ppermute | solution.py:228
  6.6 0.5 collective-permute-start.4
  7.1 0.1 collective-permute-start.3
  7.2 1.1 %copy.12.h_ref = bf16[384,768]{1,0:T(8,128)(2,1)} copy(bf16[384,768]{0,1:T(8,128)(2,1)S(1)} %fusion.4) | data formatting | bytes 1179648 | tf_op jit(solution)/shard_map/convert_element_type | solution.py:244
  8.3 12.0 %forward.1 = (bf16[384,3072]{1,0:T(8,128)(2,1)}, bf16[384,3072]{1,0:T(8,128)(2,1)}, f32[384,768]{1,0:T(8,128)}, bf16[384,768]{1,0:T(8,128)(2,1)}) custom-call(bf16[384,768]{1,0:T(8,128)(2,1)} %copy.12.h_ref, bf16[768,3072]{1,0:T(8,128)(2,1)} %bitcast.28, bf16[3072,768]{1,0:T(8,128)(2,1)} %bitcast.31, bf16[384,768]{1,0:T(8,128)(2,1)} %bitcast.39, ...), custom_call_target="tpu_custom_call" | custom-call | flops 3623878656 | bytes 14155776 | tf_op jit(solution)/shard_map/forward/pallas_call | solution.py:253
  20.3 12.1 %backward.1 = (bf16[384,3072]{1,0:T(8,128)(2,1)}, bf16[768,384]{1,0:T(8,128)(2,1)}) custom-call(bf16[384,768]{1,0:T(8,128)(2,1)} %get-tuple-element.11.mid_ref.refs_0_, bf16[3072,768]{1,0:T(8,128)(2,1)} %bitcast.32, bf16[768,3072]{1,0:T(8,128)(2,1)} %bitcast.29, bf16[384,3072]{1,0:T(8,128)(2,1)} %get-tuple-element.13.slope_ref, ...), custom_call_target="tpu_custom_call" | custom-call | flops 3623878656 | bytes 14155776 | tf_op jit(solution)/shard_map/backward/pallas_call | solution.py:270
  32.4 0.0 copy-start
  32.4 0.0 copy-start.5
  32.4 0.0 copy-start.6
  32.4 5.4 %all-to-all-start = ((bf16[8,96,384]{2,1,0:T(8,128)(2,1)}), bf16[8,96,384]{2,1,0:T(8,128)(2,1)}, u32[]{:S(2)}, u32[]{:S(2)}) async-start(bf16[8,96,384]{2,1,0:T(8,128)(2,1)} %bitcast.38), calls=%async_computation | async-start | bytes 1179648 | tf_op jit(solution)/shard_map/all_to_all | solution.py:288
  37.8 0.0 copy-done
  37.8 2.5 %collective-permute-start.2 = (bf16[384,768]{1,0:T(8,128)(2,1)S(1)}, bf16[384,768]{1,0:T(8,128)(2,1)}, u32[]{:S(2)}, u32[]{:S(2)}) collective-permute-start(bf16[384,768]{1,0:T(8,128)(2,1)S(1)} %copy-done), channel_id=1, source_target_pairs={{0,24},{8,16},{16,8},{24,0},{1,25},{9,17},{17,9},{25,1},{2,26},{10... | collective-permute-start | bytes 1769480 | tf_op jit(solution)/shard_map/ppermute | solution.py:228
  40.4 0.5 collective-permute-start.1
  40.9 0.0 copy-done.5
  40.9 0.0 copy-done.6
  40.9 0.0 collective-permute-done.5
  40.9 0.6 collective-permute-start
  41.5 1.1 %copy.15.refs_2_ = bf16[384,768]{1,0:T(8,128)(2,1)} copy(bf16[384,768]{0,1:T(8,128)(2,1)S(1)} %collective-permute-done.5) | data formatting | bytes 1179648 | tf_op jit(solution)/shard_map/ppermute | solution.py:228
  42.6 0.0 collective-permute-done.4
  42.6 1.1 %copy.14.refs_1_ = bf16[384,768]{1,0:T(8,128)(2,1)} copy(bf16[384,768]{0,1:T(8,128)(2,1)S(1)} %collective-permute-done.4) | data formatting | bytes 1179648 | tf_op jit(solution)/shard_map/ppermute | solution.py:228
  43.7 0.0 collective-permute-done.3
  43.7 1.1 %copy.13.refs_0_ = bf16[384,768]{1,0:T(8,128)(2,1)} copy(bf16[384,768]{0,1:T(8,128)(2,1)S(1)} %collective-permute-done.3) | data formatting | bytes 1179648 | tf_op jit(solution)/shard_map/ppermute | solution.py:228
  44.8 0.0 copy-start.3
  44.8 18.4 %others.1 = (bf16[3,384,3072]{2,1,0:T(8,128)(2,1)}, bf16[3,384,768]{2,1,0:T(8,128)(2,1)}) custom-call(s32[1]{0:T(128)} %bitcast.8.me_ref, bf16[384,768]{1,0:T(8,128)(2,1)} %copy.13.refs_0_, bf16[384,768]{1,0:T(8,128)(2,1)} %copy.14.refs_1_, bf16[384,768]{1,0:T(8,128)(2,1)} %copy.15.refs_2_, bf16[768,3072]{1,0:T(8,128)(2,1)} %bitcast.30), custom_call_target="tpu_custom_call" | custom-call | flops 5435817984 | bytes 14155776 | tf_op jit(solution)/shard_map/others/pallas_call | solution.py:296
  63.2 0.7 dynamic-slice_bitcast_fusion
  63.9 0.7 dynamic-slice_bitcast_fusion.1
  64.5 0.0 all-to-all-done
  64.5 0.0 copy-done.3
  64.5 3.3 %convolution_convert_fusion = bf16[1024,768]{1,0:T(8,128)(2,1)} fusion(s32[384]{0:T(512)S(1)} %fusion.8, bf16[768,384]{1,0:T(8,128)(2,1)} %bitcast.17, bf16[768,384]{1,0:T(8,128)(2,1)S(1)} %copy-done.3), kind=kOutput, calls=%fused_computation.1 | convolution fusion | flops 606339072 | bytes 2754048 | tf_op jit(solution)/shard_map/dot_general | solution.py:43
  67.8 3.7 %all-to-all-start.1 = ((bf16[4,256,768]{2,1,0:T(8,128)(2,1)}), bf16[4,256,768]{2,1,0:T(8,128)(2,1)S(1)}, u32[]{:S(2)}, u32[]{:S(2)}) async-start(bf16[4,256,768]{2,1,0:T(8,128)(2,1)} %bitcast.36), calls=%async_computation.1 | async-start | bytes 3145728 | tf_op jit(solution)/shard_map/all_to_all | solution.py:360
  71.6 0.0 collective-permute-done.2.refs_2_.refs_3_
  71.6 0.0 collective-permute-done.1.refs_1_.refs_2_
  71.6 0.0 collective-permute-done.refs_0_.refs_1_
  71.6 0.0 copy-start.1
  71.6 0.0 copy-start.2
  71.6 6.4 %downgrad.1 = f32[768,768]{1,0:T(8,128)} custom-call(s32[1]{0:T(128)} %bitcast.8.me_ref, bf16[384,3072]{1,0:T(8,128)(2,1)} %get-tuple-element.16.own_ref, bf16[3,384,768]{2,1,0:T(8,128)(2,1)} %get-tuple-element.17.act_ref, bf16[384,768]{1,0:T(8,128)(2,1)} %get-tuple-element.11.mid_ref.refs_0_, bf16[384,768]{1,0:T(8,128)(2,1)} %collective-permute-done.refs_0_.refs_1_, ...), custom_call_target="tpu_custom_call" | custom-call | flops 1811939328 | bytes 9437184 | tf_op jit(solution)/shard_map/downgrad/pallas_call | solution.py:338
  78.0 0.0 copy-done.1
  78.0 0.0 copy-done.2
  78.0 0.9 pad_maximum_fusion.refs_3_
  78.8 15.0 %upgrad.1 = f32[192,3072]{1,0:T(8,128)} custom-call(bf16[384,768]{1,0:T(8,128)(2,1)} %collective-permute-done.refs_0_.refs_1_, bf16[384,768]{1,0:T(8,128)(2,1)} %collective-permute-done.1.refs_1_.refs_2_, bf16[384,768]{1,0:T(8,128)(2,1)} %collective-permute-done.2.refs_2_.refs_3_, bf16[192,1536]{1,0:T(8,128)(2,1)} %pad_maximum_fusion.refs_3_, ...), custom_call_target="tpu_custom_call" | custom-call | flops 7247757312 | bytes 23592960 | tf_op jit(solution)/shard_map/upgrad/pallas_call | solution.py:321
  93.9 0.0 all-to-all-done.1
  93.9 1.1 %convert_reduce_fusion = f32[256,768]{1,0:T(8,128)} fusion(bf16[4,256,768]{2,1,0:T(8,128)(2,1)S(1)} %all-to-all-done.1), kind=kLoop, calls=%fused_computation | loop fusion | flops 1376256 | bytes 2359296 | tf_op jit(solution)/shard_map/reduce_sum | solution.py:361
  (6 shorter events, 0.1 us)
Async XLA Ops:
  0.6 1.8 %copy-start.4 = (f32[1,768]{1,0:T(1,128)S(1)}, f32[1,768]{1,0:T(1,128)}, u32[]{:S(2)}) copy-start(f32[1,768]{1,0:T(1,128)} %gain_ref.3) | copy-start | bytes 9220
  2.6 38.3 %collective-permute-start.5 = (bf16[384,768]{0,1:T(8,128)(2,1)S(1)}, bf16[384,768]{0,1:T(8,128)(2,1)S(1)}, u32[]{:S(2)}, u32[]{:S(2)}) collective-permute-start(bf16[384,768]{0,1:T(8,128)(2,1)S(1)} %fusion.4), channel_id=1, source_target_pairs={{0,24},{8,16},{16,8},{24,0},{1,25},{9,17},{17,9},{25,1},{2,26},{10... | collective-permute-start | bytes 1769480 | tf_op jit(solution)/shard_map/ppermute | solution.py:228
  6.6 36.0 %collective-permute-start.4 = (bf16[384,768]{0,1:T(8,128)(2,1)S(1)}, bf16[384,768]{0,1:T(8,128)(2,1)S(1)}, u32[]{:S(2)}, u32[]{:S(2)}) collective-permute-start(bf16[384,768]{0,1:T(8,128)(2,1)S(1)} %fusion.4), channel_id=1, source_target_pairs={{0,16},{8,24},{16,0},{24,8},{1,17},{9,25},{17,1},{25,9},{2,18},{10... | collective-permute-start | bytes 1769480 | tf_op jit(solution)/shard_map/ppermute | solution.py:228
  7.1 36.6 %collective-permute-start.3 = (bf16[384,768]{0,1:T(8,128)(2,1)S(1)}, bf16[384,768]{0,1:T(8,128)(2,1)S(1)}, u32[]{:S(2)}, u32[]{:S(2)}) collective-permute-start(bf16[384,768]{0,1:T(8,128)(2,1)S(1)} %fusion.4), channel_id=1, source_target_pairs={{0,8},{8,0},{16,24},{24,16},{1,9},{9,1},{17,25},{25,17},{2,10},{10... | collective-permute-start | bytes 1769480 | tf_op jit(solution)/shard_map/ppermute | solution.py:228
  32.4 5.5 %copy-start = (bf16[384,768]{1,0:T(8,128)(2,1)S(1)}, bf16[384,768]{1,0:T(8,128)(2,1)}, u32[]{:S(2)}) copy-start(bf16[384,768]{1,0:T(8,128)(2,1)} %get-tuple-element.11.mid_ref.refs_0_) | copy-start | bytes 1769476
  32.4 8.5 %copy-start.5 = (s32[1,384]{1,0:T(1,128)S(1)}, s32[1,384]{1,0:T(1,128)}, u32[]{:S(2)}) copy-start(s32[1,384]{1,0:T(1,128)} %param.15) | copy-start | bytes 4612
  32.4 8.5 %copy-start.6 = (s32[1,384,1]{1,2,0:T(1,128)S(1)}, s32[1,384,1]{1,2,0:T(1,128)}, u32[]{:S(2)}) copy-start(s32[1,384,1]{1,2,0:T(1,128)} %param.14) | copy-start | bytes 4612
  32.4 32.1 %all-to-all-start = ((bf16[8,96,384]{2,1,0:T(8,128)(2,1)}), bf16[8,96,384]{2,1,0:T(8,128)(2,1)}, u32[]{:S(2)}, u32[]{:S(2)}) async-start(bf16[8,96,384]{2,1,0:T(8,128)(2,1)} %bitcast.38), calls=%async_computation | async-start | bytes 1179648 | tf_op jit(solution)/shard_map/all_to_all | solution.py:288
  37.8 33.7 %collective-permute-start.2 = (bf16[384,768]{1,0:T(8,128)(2,1)S(1)}, bf16[384,768]{1,0:T(8,128)(2,1)}, u32[]{:S(2)}, u32[]{:S(2)}) collective-permute-start(bf16[384,768]{1,0:T(8,128)(2,1)S(1)} %copy-done), channel_id=1, source_target_pairs={{0,24},{8,16},{16,8},{24,0},{1,25},{9,17},{17,9},{25,1},{2,26},{10... | collective-permute-start | bytes 1769480 | tf_op jit(solution)/shard_map/ppermute | solution.py:228
  40.4 31.2 %collective-permute-start.1 = (bf16[384,768]{1,0:T(8,128)(2,1)S(1)}, bf16[384,768]{1,0:T(8,128)(2,1)}, u32[]{:S(2)}, u32[]{:S(2)}) collective-permute-start(bf16[384,768]{1,0:T(8,128)(2,1)S(1)} %copy-done), channel_id=1, source_target_pairs={{0,16},{8,24},{16,0},{24,8},{1,17},{9,25},{17,1},{25,9},{2,18},{10... | collective-permute-start | bytes 1769480 | tf_op jit(solution)/shard_map/ppermute | solution.py:228
  40.9 30.6 %collective-permute-start = (bf16[384,768]{1,0:T(8,128)(2,1)S(1)}, bf16[384,768]{1,0:T(8,128)(2,1)}, u32[]{:S(2)}, u32[]{:S(2)}) collective-permute-start(bf16[384,768]{1,0:T(8,128)(2,1)S(1)} %copy-done), channel_id=1, source_target_pairs={{0,8},{8,0},{16,24},{24,16},{1,9},{9,1},{17,25},{25,17},{2,10},{10... | collective-permute-start | bytes 1769480 | tf_op jit(solution)/shard_map/ppermute | solution.py:228
  44.8 19.8 %copy-start.3 = (bf16[768,384]{1,0:T(8,128)(2,1)S(1)}, bf16[768,384]{1,0:T(8,128)(2,1)}, u32[]{:S(2)}) copy-start(bf16[768,384]{1,0:T(8,128)(2,1)} %get-tuple-element.18) | copy-start | bytes 1769476
  67.8 26.0 %all-to-all-start.1 = ((bf16[4,256,768]{2,1,0:T(8,128)(2,1)}), bf16[4,256,768]{2,1,0:T(8,128)(2,1)S(1)}, u32[]{:S(2)}, u32[]{:S(2)}) async-start(bf16[4,256,768]{2,1,0:T(8,128)(2,1)} %bitcast.36), calls=%async_computation.1 | async-start | bytes 3145728 | tf_op jit(solution)/shard_map/all_to_all | solution.py:360
  71.6 6.4 %copy-start.1 = (bf16[192,384]{1,0:T(8,128)(2,1)S(1)}, bf16[192,384]{1,0:T(8,128)(2,1)}, u32[]{:S(2)}) copy-start(bf16[192,384]{1,0:T(8,128)(2,1)} %dynamic-slice_bitcast_fusion) | copy-start | bytes 442372
  71.6 6.4 %copy-start.2 = (bf16[192,384]{1,0:T(8,128)(2,1)S(1)}, bf16[192,384]{1,0:T(8,128)(2,1)}, u32[]{:S(2)}) copy-start(bf16[192,384]{1,0:T(8,128)(2,1)} %dynamic-slice_bitcast_fusion.1) | copy-start | bytes 442372

commit v2 on v1

--- a/solution.py
+++ b/solution.py
@@ -5,6 +5,7 @@
 from jax import lax
 from jax.experimental import pallas as pl
 from jax.experimental.pallas import tpu as pltpu
+
 from jax.sharding import PartitionSpec as P
 
 HOT = 256
@@ -119,7 +120,9 @@
     return (grad_up[None], grad_down[None], row_grad[None])
 
 
-TILE = 512
+TILE = 1536
+SUB = 256
+TILE_U = 1024
 VMEM_BYTES = 60 * 1024 * 1024
 
 
@@ -129,22 +132,31 @@
     )
 
 
+def norm_kernel(mix_ref, gain_ref, out_ref):
+    normed, _ = normalize(mix_ref[...].astype(jnp.float32))
+    out_ref[...] = (normed * gain_ref[...]).astype(jnp.bfloat16)
+
+
 def forward_kernel(h_ref, up_ref, down_ref, grad_ref, gain_ref, act_ref, slope_ref, wide_ref, mid_ref, acc):
     step = pl.program_id(0)
-    pre = jnp.dot(h_ref[...], up_ref[...], preferred_element_type=jnp.float32)
-    value, slope = gelu_parts(pre)
-    act = value.astype(jnp.bfloat16)
-    act_ref[...] = act
-    slope_ref[...] = slope.astype(jnp.bfloat16)
-    part = jnp.dot(act, down_ref[...], preferred_element_type=jnp.float32)
 
     @pl.when(step == 0)
     def _():
-        acc[...] = part + h_ref[...].astype(jnp.float32)
-
-    @pl.when(step > 0)
-    def _():
-        acc[...] += part
+        acc[...] = h_ref[...].astype(jnp.float32)
+
+    pres = []
+    for s in range(0, act_ref.shape[1], SUB):
+        pres.append(jnp.dot(h_ref[...], up_ref[:, s : s + SUB], preferred_element_type=jnp.float32))
+    part = None
+    for i, pre in enumerate(pres):
+        cols = slice(i * SUB, (i + 1) * SUB)
+        value, slope = gelu_parts(pre)
+        act = value.astype(jnp.bfloat16)
+        act_ref[:, cols] = act
+        slope_ref[:, cols] = slope.astype(jnp.bfloat16)
+        more = jnp.dot(act, down_ref[cols, :], preferred_element_type=jnp.float32)
+        part = more if part is None else part + more
+    acc[...] += part
 
     @pl.when(step == pl.num_programs(0) - 1)
     def _():
@@ -156,18 +168,15 @@
 
 def backward_kernel(mid_ref, down_ref, up_ref, slope_ref, wide_ref, mix_ref, gain_ref, pre_ref, sum_ref, acc):
     step = pl.program_id(0)
+
+    @pl.when(step == 0)
+    def _():
+        acc[...] = wide_ref[...]
+
     grad_act = contract_cols(mid_ref[...], down_ref[...])
     grad_pre = (grad_act * slope_ref[...].astype(jnp.float32)).astype(jnp.bfloat16)
     pre_ref[...] = grad_pre
-    part = contract_cols(grad_pre, up_ref[...])
-
-    @pl.when(step == 0)
-    def _():
-        acc[...] = part + wide_ref[...]
-
-    @pl.when(step > 0)
-    def _():
-        acc[...] += part
+    acc[...] += contract_cols(grad_pre, up_ref[...])
 
     @pl.when(step == pl.num_programs(0) - 1)
     def _():
@@ -176,30 +185,35 @@
         sum_ref[...] = grad_sum.T.astype(jnp.bfloat16)
 
 
-def others_kernel(own_tiles, me_ref, *refs):
+def others_kernel(me_ref, *refs):
     h_refs = refs[: len(refs) - 3]
     up_ref, slope_ref, act_ref = refs[len(refs) - 3 :]
     for g, h_ref in enumerate(h_refs):
         pre = jnp.dot(h_ref[...], up_ref[...], preferred_element_type=jnp.float32)
         value, slope = gelu_parts(pre)
         slope_ref[g] = slope.astype(jnp.bfloat16)
-
-        @pl.when(pl.program_id(0) < own_tiles)
-        def _():
-            act_ref[g] = value.astype(jnp.bfloat16)
-
-
-def up_kernel(groups, *refs):
+        act_ref[g] = value.astype(jnp.bfloat16)
+
+
+def up_kernel(groups, me_ref, *refs):
     mid_refs = refs[: groups - 1]
-    hsel_ref, down_ref, slope_ref, own_ref, up_ref = refs[groups - 1 :]
-    rows = own_ref.shape[0]
-    total = jnp.dot(hsel_ref[:, :rows], own_ref[...], preferred_element_type=jnp.float32)
+    h_refs = refs[groups - 1 : 2 * groups - 1]
+    down_ref, slope_ref, own_ref, up_ref, hsel = refs[2 * groups - 1 :]
+    width = h_refs[0].shape[1]
+    out_rows = up_ref.shape[0]
+
+    @pl.when(pl.program_id(0) == 0)
+    def _():
+        row = lax.broadcasted_iota(jnp.int32, (out_rows, width), 0) + me_ref[0] * out_rows
+        pick = (row == lax.broadcasted_iota(jnp.int32, (out_rows, width), 1)).astype(jnp.bfloat16)
+        for g, h_ref in enumerate(h_refs):
+            hsel[g] = contract_cols(pick, h_ref[...]).astype(jnp.bfloat16)
+
+    total = jnp.dot(hsel[0], own_ref[...], preferred_element_type=jnp.float32)
     for g in range(groups - 1):
         grad_act = contract_cols(mid_refs[g][...], down_ref[...])
         grad_pre = (grad_act * slope_ref[g].astype(jnp.float32)).astype(jnp.bfloat16)
-        total += jnp.dot(
-            hsel_ref[:, (g + 1) * rows : (g + 2) * rows], grad_pre, preferred_element_type=jnp.float32
-        )
+        total += jnp.dot(hsel[g + 1], grad_pre, preferred_element_type=jnp.float32)
     up_ref[...] = total
 
 
@@ -224,9 +238,10 @@
 
 
 def gather_groups(value, groups):
-    return [
-        lax.ppermute(value, "dp", [(i, i ^ k) for i in range(groups)]) for k in range(1, groups)
-    ]
+    taken = []
+    for k in range(1, groups):
+        taken.append(lax.ppermute(value, "dp", [(i, i ^ k) for i in range(groups)]))
+    return taken
 
 
 def small_group(mix_input, out_grad, w_up, w_down, gain_first, gain_second, owner_dev, slot_row):
@@ -240,8 +255,12 @@
     up_mat, down_mat = w_up[0], w_down[0]
     mix = mix_input[:, 0, :]
     grad = out_grad[:, 0, :]
-    normed, _ = normalize(mix.astype(jnp.float32))
-    hidden_in = (normed * gain_first[0]).astype(jnp.bfloat16)
+    hidden_in = pl.pallas_call(
+        norm_kernel,
+        out_shape=jax.ShapeDtypeStruct((rows, width), jnp.bfloat16),
+        compiler_params=params(),
+        name="norm",
+    )(mix, gain_first)
     others_h = gather_groups(hidden_in, groups)
     steps = hidden // TILE
     bf, f32 = jnp.bfloat16, jnp.float32
@@ -290,19 +309,19 @@
     ).reshape(width, rows)
 
     own_cols = hidden // groups
-    tile_a = min(TILE, own_cols // 2)
+    tile_a = own_cols
     own_tiles = own_cols // tile_a
     steps_a = hidden // tile_a
     o_slope, o_act = pl.pallas_call(
-        functools.partial(others_kernel, own_tiles),
+        others_kernel,
         grid_spec=pltpu.PrefetchScalarGridSpec(
             num_scalar_prefetch=1,
             grid=(steps_a,),
             in_specs=[whole(rows, width)] * (groups - 1)
-            + [pl.BlockSpec((width, tile_a), lambda f, m: (0, lax.rem(f + m[0] * own_tiles, steps_a)))],
+            + [pl.BlockSpec((width, tile_a), lambda f, m: (0, lax.rem(f + (m[0] + 1) * own_tiles, steps_a)))],
             out_specs=[
-                pl.BlockSpec((groups - 1, rows, tile_a), lambda f, m: (0, 0, lax.rem(f + m[0] * own_tiles, steps_a))),
-                pl.BlockSpec((groups - 1, rows, tile_a), lambda f, m: (0, 0, jnp.minimum(f, own_tiles - 1))),
+                pl.BlockSpec((groups - 1, rows, tile_a), lambda f, m: (0, 0, lax.rem(f + (m[0] + 1) * own_tiles, steps_a))),
+                pl.BlockSpec((groups - 1, rows, tile_a), lambda f, m: (0, 0, jnp.maximum(f + own_tiles - steps_a, 0))),
             ],
         ),
         out_shape=[
@@ -315,23 +334,25 @@
     )(me_arr, *others_h, up_mat)
 
     out_rows = width // groups
-    hsel = jnp.concatenate(
-        [lax.dynamic_slice(h, (0, me * out_rows), (rows, out_rows)).T for h in [hidden_in] + others_h], axis=1
-    )
     grad_up = pl.pallas_call(
         functools.partial(up_kernel, groups),
-        grid=(steps,),
-        in_specs=[whole(rows, width)] * (groups - 1)
-        + [
-            whole(out_rows, groups * rows), down_spec,
-            pl.BlockSpec((groups - 1, rows, TILE), lambda f: (0, 0, f)), col_spec,
-        ],
-        out_specs=pl.BlockSpec((out_rows, TILE), lambda f: (0, f)),
+        grid_spec=pltpu.PrefetchScalarGridSpec(
+            num_scalar_prefetch=1,
+            grid=(hidden // TILE_U,),
+            in_specs=[whole(rows, width)] * (2 * groups - 1)
+            + [
+                pl.BlockSpec((TILE_U, width), lambda f, m: (f, 0)),
+                pl.BlockSpec((groups - 1, rows, TILE_U), lambda f, m: (0, 0, f)),
+                pl.BlockSpec((rows, TILE_U), lambda f, m: (0, f)),
+            ],
+            out_specs=pl.BlockSpec((out_rows, TILE_U), lambda f, m: (0, f)),
+            scratch_shapes=[pltpu.VMEM((groups, out_rows, rows), bf)],
+        ),
         out_shape=jax.ShapeDtypeStruct((out_rows, hidden), f32),
         compiler_params=params(),
         cost_estimate=cost(groups * unit, 5 * wbytes),
         name="upgrad",
-    )(*others_mid, hsel, down_mat, o_slope, grad_pre)
+    )(me_arr, *others_mid, hidden_in, *others_h, down_mat, o_slope, grad_pre)
 
     part = own_cols // 3 if own_cols % 384 == 0 else own_cols
     parts = own_cols // part
@@ -373,8 +394,13 @@
         P("token", "dp", None),
         P("token", "dp"),
     )
+    small = mesh.shape["dp"] <= 4
+
+    def layer(*args):
+        return (small_group if small else per_device)(*args)
+
     return jax.shard_map(
-        small_group if mesh.shape["dp"] <= 4 else per_device,
+        layer,
         mesh=mesh,
         in_specs=placed,
         out_specs=(P("token", "dp", None), P("token", "dp", None), P("token", "dp", None)),

time: 95.6 us -> 109 us (1.14)
  waiting for transfers between devices: 0.02 us -> 27.7 us
  Pallas kernels: 63.8 us -> 56.9 us
  local copies, waits for them, and re-layouts: 7.11 us -> 0.67 us
  other arithmetic: 2.56 us -> 1.11 us
    ppermute x6, waiting for transfers between devices: 0.02 us -> 27.7 us  [gather_groups(): taken.append(lax.ppermute(value, 'dp', [(i, i ^ k) for i in range(groups)]))]
    pallas_call x2 -> x3, Pallas kernels: 33.4 us -> 29.9 us  [the longest x1 14.9 us: small_group(): pl.pallas_call(functools.partial(up_kernel, groups), grid_spec=pltpu.Pref...]
    ppermute x3 -> x0, local copies, waits for them, and re-layouts: 3.23 us -> none  [gather_groups(): lax.ppermute(value, 'dp', [(i, i ^ k) for i in range(groups)])]
    pallas_call x1, Pallas kernels: 12 us -> 9.99 us  [small_group(): pl.pallas_call(forward_kernel, grid=(steps,), in_specs=[whole(rows, width...]
    transpose x4 -> x0, local copies, waits for them, and re-layouts: 1.39 us -> none  [small_group(): lax.dynamic_slice(h, (0, me * out_rows), (rows, out_rows))]
    pallas_call x1, Pallas kernels: 12.1 us -> 10.7 us  [small_group(): pl.pallas_call(backward_kernel, grid=(steps,), in_specs=[whole(rows, widt...]
  transfers between devices with their start and end apart: 8 -> 8, of which waited for: 0 -> 4; matrix products, arithmetic and copies ran while one was open for 10% -> 3% of each run, Pallas kernels for 67% -> 31%
where the time goes in v2:
time: 109 us; the launch traced here: 108 us
  Pallas kernels  56.9 us (52%)
  waiting for transfers between devices  27.7 us (25%)
  starting transfers between devices  18 us (17%)
  matrix products  3.3 us (3%)
  other arithmetic  1.11 us (1%)
    ppermute x6, waiting for transfers between devices, gather_groups(): taken.append(lax.ppermute(value, 'dp', [(i, i ^ k) for i in range(groups)]))  27.7 us
    pallas_call x1, Pallas kernels, small_group(): pl.pallas_call(functools.partial(up_kernel, groups), grid_spec=pltpu.Pref...  14.9 us
    pallas_call x1, Pallas kernels, small_group(): pl.pallas_call(others_kernel, grid_spec=pltpu.PrefetchScalarGridSpec(num_...  12.7 us
    pallas_call x1, Pallas kernels, small_group(): pl.pallas_call(backward_kernel, grid=(steps,), in_specs=[whole(rows, widt...  10.7 us
    pallas_call x1, Pallas kernels, small_group(): pl.pallas_call(forward_kernel, grid=(steps,), in_specs=[whole(rows, width...  9.99 us
    ppermute x6, starting transfers between devices, gather_groups(): taken.append(lax.ppermute(value, 'dp', [(i, i ^ k) for i in range(groups)]))  7.93 us
    all_to_all x1, starting transfers between devices, small_group(): lax.all_to_all(sum_t.reshape(pieces, width // pieces, rows), 'token', spl...  6.36 us
    pallas_call x1, Pallas kernels, small_group(): pl.pallas_call(down_kernel, grid_spec=pltpu.PrefetchScalarGridSpec(num_sc...  6.26 us
  transfers between devices with their start and end apart: 8, of which 4 were waited for; matrix products, arithmetic and copies ran while one was open for 3% of the time, Pallas kernels for 31%

profile of v2, /device:TPU:0, one launch (start us, length us, event | category | flops | bytes accessed | tf_op | source)
XLA Modules:
  0.0 108.4 jit_solution(17782974812516551423)
XLA Ops:
  0.6 2.3 %norm.1.h_ref.refs_3_ = bf16[384,768]{1,0:T(8,128)(2,1)} custom-call(bf16[384,768]{1,0:T(8,128)(2,1)} %bitcast.23, f32[1,768]{1,0:T(1,128)} %gain_ref.5), custom_call_target="tpu_custom_call" | custom-call | tf_op jit(solution)/shard_map/norm/pallas_call | solution.py:258
  2.9 10.0 %forward.1 = (bf16[384,3072]{1,0:T(8,128)(2,1)}, bf16[384,3072]{1,0:T(8,128)(2,1)}, f32[384,768]{1,0:T(8,128)}, bf16[384,768]{1,0:T(8,128)(2,1)}) custom-call(bf16[384,768]{1,0:T(8,128)(2,1)} %norm.1.h_ref.refs_3_, bf16[768,3072]{1,0:T(8,128)(2,1)} %bitcast.16, bf16[3072,768]{1,0:T(8,128)(2,1)} %bitcast.19, bf16[384,768]{1,0:T(8,128)(2,1)} %bitcast.29, ...), custom_call_target="tpu_custom_call" | custom-call | flops 3623878656 | bytes 14155776 | tf_op jit(solution)/shard_map/forward/pallas_call | solution.py:272
  12.9 0.0 copy-start
  12.9 0.0 copy-start.3
  12.9 0.0 copy-start.4
  12.9 10.7 %backward.1 = (bf16[384,3072]{1,0:T(8,128)(2,1)}, bf16[768,384]{1,0:T(8,128)(2,1)}) custom-call(bf16[384,768]{1,0:T(8,128)(2,1)} %get-tuple-element.11.mid_ref.refs_0_, bf16[3072,768]{1,0:T(8,128)(2,1)} %bitcast.20, bf16[768,3072]{1,0:T(8,128)(2,1)} %bitcast.17, bf16[384,3072]{1,0:T(8,128)(2,1)} %get-tuple-element.13.slope_ref, ...), custom_call_target="tpu_custom_call" | custom-call | flops 3623878656 | bytes 14155776 | tf_op jit(solution)/shard_map/backward/pallas_call | solution.py:289
  23.6 6.4 %all-to-all-start = ((bf16[8,96,384]{2,1,0:T(8,128)(2,1)}), bf16[8,96,384]{2,1,0:T(8,128)(2,1)S(1)}, u32[]{:S(2)}, u32[]{:S(2)}) async-start(bf16[8,96,384]{2,1,0:T(8,128)(2,1)} %bitcast.27), calls=%async_computation | async-start | bytes 1179648 | tf_op jit(solution)/shard_map/all_to_all | solution.py:307
  30.0 2.4 %collective-permute-start.5 = (bf16[384,768]{1,0:T(8,128)(2,1)}, bf16[384,768]{1,0:T(8,128)(2,1)S(1)}, u32[]{:S(2)}, u32[]{:S(2)}) collective-permute-start(bf16[384,768]{1,0:T(8,128)(2,1)} %norm.1.h_ref.refs_3_), channel_id=1, source_target_pairs={{0,24},{8,16},{16,8},{24,0},{1,25},{9,17},{17,9},{25,1},{2,26},{10... | collective-permute-start | bytes 1769480 | tf_op jit(solution)/shard_map/ppermute | solution.py:243
  32.4 0.5 collective-permute-start.4
  32.9 0.5 collective-permute-start.3
  33.5 0.0 copy-done
  33.5 2.4 %collective-permute-start.2 = (bf16[384,768]{1,0:T(8,128)(2,1)S(1)}, bf16[384,768]{1,0:T(8,128)(2,1)S(1)}, u32[]{:S(2)}, u32[]{:S(2)}) collective-permute-start(bf16[384,768]{1,0:T(8,128)(2,1)S(1)} %copy-done), channel_id=1, source_target_pairs={{0,24},{8,16},{16,8},{24,0},{1,25},{9,17},{17,9},{25,1},{2,26},{10... | collective-permute-start | bytes 1769480 | tf_op jit(solution)/shard_map/ppermute | solution.py:243
  35.9 0.5 collective-permute-start.1
  36.4 0.0 copy-done.3
  36.4 0.0 copy-done.4
  36.5 10.9 %collective-permute-done.5.refs_2_.refs_6_ = bf16[384,768]{1,0:T(8,128)(2,1)S(1)} collective-permute-done((bf16[384,768]{1,0:T(8,128)(2,1)}, bf16[384,768]{1,0:T(8,128)(2,1)S(1)}, u32[]{:S(2)}, u32[]{:S(2)}) %collective-permute-start.5) | collective-permute-done | bytes 589856 | tf_op jit(solution)/shard_map/ppermute | solution.py:243
  47.3 0.0 copy-start.5
  47.3 1.5 %collective-permute-start = (bf16[384,768]{1,0:T(8,128)(2,1)S(1)}, bf16[384,768]{1,0:T(8,128)(2,1)}, u32[]{:S(2)}, u32[]{:S(2)}) collective-permute-start(bf16[384,768]{1,0:T(8,128)(2,1)S(1)} %copy-done), channel_id=1, source_target_pairs={{0,8},{8,0},{16,24},{24,16},{1,9},{9,1},{17,25},{25,17},{2,10},{10... | collective-permute-start | bytes 1769480 | tf_op jit(solution)/shard_map/ppermute | solution.py:243
  48.8 0.0 all-to-all-done
  48.8 3.3 %convolution_convert_fusion = bf16[1024,768]{1,0:T(8,128)(2,1)} fusion(s32[384]{0:T(512)S(1)} %fusion.3, bf16[768,384]{1,0:T(8,128)(2,1)S(1)} %bitcast.28, bf16[768,384]{1,0:T(8,128)(2,1)} %get-tuple-element.18), kind=kOutput, calls=%fused_computation.1 | convolution fusion | flops 606339072 | bytes 2754048 | tf_op jit(solution)/shard_map/dot_general | solution.py:44
  52.1 0.0 copy-done.5
  52.1 3.7 %all-to-all-start.1 = ((bf16[4,256,768]{2,1,0:T(8,128)(2,1)}), bf16[4,256,768]{2,1,0:T(8,128)(2,1)S(1)}, u32[]{:S(2)}, u32[]{:S(2)}) async-start(bf16[4,256,768]{2,1,0:T(8,128)(2,1)} %bitcast.25), calls=%async_computation.1 | async-start | bytes 3145728 | tf_op jit(solution)/shard_map/all_to_all | solution.py:381
  55.9 4.2 %collective-permute-done.4.refs_1_.refs_5_ = bf16[384,768]{1,0:T(8,128)(2,1)} collective-permute-done((bf16[384,768]{1,0:T(8,128)(2,1)}, bf16[384,768]{1,0:T(8,128)(2,1)}, u32[]{:S(2)}, u32[]{:S(2)}) %collective-permute-start.4) | collective-permute-done | bytes 589856 | tf_op jit(solution)/shard_map/ppermute | solution.py:243
  60.1 0.0 collective-permute-done.3.refs_0_.refs_4_
  60.1 12.7 %others.1 = (bf16[3,384,3072]{2,1,0:T(8,128)(2,1)}, bf16[3,384,768]{2,1,0:T(8,128)(2,1)}) custom-call(s32[1]{0:T(128)} %bitcast.me_ref, bf16[384,768]{1,0:T(8,128)(2,1)} %collective-permute-done.3.refs_0_.refs_4_, bf16[384,768]{1,0:T(8,128)(2,1)} %collective-permute-done.4.refs_1_.refs_5_, bf16[384,768]{1,0:T(8,128)(2,1)} %copy-done.5, ...), custom_call_target="tpu_custom_call" | custom-call | flops 5435817984 | bytes 14155776 | tf_op jit(solution)/shard_map/others/pallas_call | solution.py:315
  72.9 0.0 collective-permute-done.2.refs_2_.refs_3_
  72.9 0.0 copy-start.1
  72.9 12.4 %collective-permute-done.1.refs_1_.refs_2_ = bf16[384,768]{1,0:T(8,128)(2,1)S(1)} collective-permute-done((bf16[384,768]{1,0:T(8,128)(2,1)S(1)}, bf16[384,768]{1,0:T(8,128)(2,1)S(1)}, u32[]{:S(2)}, u32[]{:S(2)}) %collective-permute-start.1) | collective-permute-done | bytes 589856 | tf_op jit(solution)/shard_map/ppermute | solution.py:243
  85.3 0.0 copy-start.2
  85.3 0.2 collective-permute-done.refs_0_.refs_1_
  85.5 0.0 copy-done.1
  85.5 0.6 copy-done.2
  86.1 6.3 %downgrad.1 = f32[768,768]{1,0:T(8,128)} custom-call(s32[1]{0:T(128)} %bitcast.me_ref, bf16[384,3072]{1,0:T(8,128)(2,1)} %get-tuple-element.16.own_ref, bf16[3,384,768]{2,1,0:T(8,128)(2,1)} %get-tuple-element.17.act_ref, bf16[384,768]{1,0:T(8,128)(2,1)} %get-tuple-element.11.mid_ref.refs_0_, bf16[384,768]{1,0:T(8,128)(2,1)} %collective-permute-done.refs_0_.refs_1_, ...), custom_call_target="tpu_custom_call" | custom-call | flops 1811939328 | bytes 9437184 | tf_op jit(solution)/shard_map/downgrad/pallas_call | solution.py:359
  92.4 14.9 %upgrad.1 = f32[192,3072]{1,0:T(8,128)} custom-call(s32[1]{0:T(128)} %bitcast.me_ref, bf16[384,768]{1,0:T(8,128)(2,1)} %collective-permute-done.refs_0_.refs_1_, bf16[384,768]{1,0:T(8,128)(2,1)} %copy-done.2, bf16[384,768]{1,0:T(8,128)(2,1)} %copy-done.1, bf16[384,768]{1,0:T(8,128)(2,1)} %norm.1.h_ref.refs_3_, ...), custom_call_target="tpu_custom_call" | custom-call | flops 7247757312 | bytes 23592960 | tf_op jit(solution)/shard_map/upgrad/pallas_call | solution.py:337
  107.3 0.0 all-to-all-done.1
  107.3 1.1 %convert_reduce_fusion = f32[256,768]{1,0:T(8,128)} fusion(bf16[4,256,768]{2,1,0:T(8,128)(2,1)S(1)} %all-to-all-done.1), kind=kLoop, calls=%fused_computation | loop fusion | flops 1376256 | bytes 2359296 | tf_op jit(solution)/shard_map/reduce_sum | solution.py:382
  (1 shorter events, 0.0 us)
Async XLA Ops:
  12.9 20.6 %copy-start = (bf16[384,768]{1,0:T(8,128)(2,1)S(1)}, bf16[384,768]{1,0:T(8,128)(2,1)}, u32[]{:S(2)}) copy-start(bf16[384,768]{1,0:T(8,128)(2,1)} %get-tuple-element.11.mid_ref.refs_0_) | copy-start | bytes 1769476
  12.9 23.5 %copy-start.3 = (s32[1,384]{1,0:T(1,128)S(1)}, s32[1,384]{1,0:T(1,128)}, u32[]{:S(2)}) copy-start(s32[1,384]{1,0:T(1,128)} %param.15) | copy-start | bytes 4612
  12.9 23.5 %copy-start.4 = (s32[1,384,1]{1,2,0:T(1,128)S(1)}, s32[1,384,1]{1,2,0:T(1,128)}, u32[]{:S(2)}) copy-start(s32[1,384,1]{1,2,0:T(1,128)} %param.14) | copy-start | bytes 4612
  23.6 25.2 %all-to-all-start = ((bf16[8,96,384]{2,1,0:T(8,128)(2,1)}), bf16[8,96,384]{2,1,0:T(8,128)(2,1)S(1)}, u32[]{:S(2)}, u32[]{:S(2)}) async-start(bf16[8,96,384]{2,1,0:T(8,128)(2,1)} %bitcast.27), calls=%async_computation | async-start | bytes 1179648 | tf_op jit(solution)/shard_map/all_to_all | solution.py:307
  30.0 17.4 %collective-permute-start.5 = (bf16[384,768]{1,0:T(8,128)(2,1)}, bf16[384,768]{1,0:T(8,128)(2,1)S(1)}, u32[]{:S(2)}, u32[]{:S(2)}) collective-permute-start(bf16[384,768]{1,0:T(8,128)(2,1)} %norm.1.h_ref.refs_3_), channel_id=1, source_target_pairs={{0,24},{8,16},{16,8},{24,0},{1,25},{9,17},{17,9},{25,1},{2,26},{10... | collective-permute-start | bytes 1769480 | tf_op jit(solution)/shard_map/ppermute | solution.py:243
  32.4 27.7 %collective-permute-start.4 = (bf16[384,768]{1,0:T(8,128)(2,1)}, bf16[384,768]{1,0:T(8,128)(2,1)}, u32[]{:S(2)}, u32[]{:S(2)}) collective-permute-start(bf16[384,768]{1,0:T(8,128)(2,1)} %norm.1.h_ref.refs_3_), channel_id=1, source_target_pairs={{0,16},{8,24},{16,0},{24,8},{1,17},{9,25},{17,1},{25,9},{2,18},{10... | collective-permute-start | bytes 1769480 | tf_op jit(solution)/shard_map/ppermute | solution.py:243
  32.9 27.2 %collective-permute-start.3 = (bf16[384,768]{1,0:T(8,128)(2,1)}, bf16[384,768]{1,0:T(8,128)(2,1)}, u32[]{:S(2)}, u32[]{:S(2)}) collective-permute-start(bf16[384,768]{1,0:T(8,128)(2,1)} %norm.1.h_ref.refs_3_), channel_id=1, source_target_pairs={{0,8},{8,0},{16,24},{24,16},{1,9},{9,1},{17,25},{25,17},{2,10},{10... | collective-permute-start | bytes 1769480 | tf_op jit(solution)/shard_map/ppermute | solution.py:243
  33.5 39.4 %collective-permute-start.2 = (bf16[384,768]{1,0:T(8,128)(2,1)S(1)}, bf16[384,768]{1,0:T(8,128)(2,1)S(1)}, u32[]{:S(2)}, u32[]{:S(2)}) collective-permute-start(bf16[384,768]{1,0:T(8,128)(2,1)S(1)} %copy-done), channel_id=1, source_target_pairs={{0,24},{8,16},{16,8},{24,0},{1,25},{9,17},{17,9},{25,1},{2,26},{10... | collective-permute-start | bytes 1769480 | tf_op jit(solution)/shard_map/ppermute | solution.py:243
  35.9 49.3 %collective-permute-start.1 = (bf16[384,768]{1,0:T(8,128)(2,1)S(1)}, bf16[384,768]{1,0:T(8,128)(2,1)S(1)}, u32[]{:S(2)}, u32[]{:S(2)}) collective-permute-start(bf16[384,768]{1,0:T(8,128)(2,1)S(1)} %copy-done), channel_id=1, source_target_pairs={{0,16},{8,24},{16,0},{24,8},{1,17},{9,25},{17,1},{25,9},{2,18},{10... | collective-permute-start | bytes 1769480 | tf_op jit(solution)/shard_map/ppermute | solution.py:243
  47.3 4.8 %copy-start.5 = (bf16[384,768]{1,0:T(8,128)(2,1)}, bf16[384,768]{1,0:T(8,128)(2,1)S(1)}, u32[]{:S(2)}) copy-start(bf16[384,768]{1,0:T(8,128)(2,1)S(1)} %collective-permute-done.5.refs_2_.refs_6_) | copy-start | bytes 1769476
  47.3 38.1 %collective-permute-start = (bf16[384,768]{1,0:T(8,128)(2,1)S(1)}, bf16[384,768]{1,0:T(8,128)(2,1)}, u32[]{:S(2)}, u32[]{:S(2)}) collective-permute-start(bf16[384,768]{1,0:T(8,128)(2,1)S(1)} %copy-done), channel_id=1, source_target_pairs={{0,8},{8,0},{16,24},{24,16},{1,9},{9,1},{17,25},{25,17},{2,10},{10... | collective-permute-start | bytes 1769480 | tf_op jit(solution)/shard_map/ppermute | solution.py:243
  52.1 55.2 %all-to-all-start.1 = ((bf16[4,256,768]{2,1,0:T(8,128)(2,1)}), bf16[4,256,768]{2,1,0:T(8,128)(2,1)S(1)}, u32[]{:S(2)}, u32[]{:S(2)}) async-start(bf16[4,256,768]{2,1,0:T(8,128)(2,1)} %bitcast.25), calls=%async_computation.1 | async-start | bytes 3145728 | tf_op jit(solution)/shard_map/all_to_all | solution.py:381
  72.9 12.6 %copy-start.1 = (bf16[384,768]{1,0:T(8,128)(2,1)}, bf16[384,768]{1,0:T(8,128)(2,1)S(1)}, u32[]{:S(2)}) copy-start(bf16[384,768]{1,0:T(8,128)(2,1)S(1)} %collective-permute-done.2.refs_2_.refs_3_) | copy-start | bytes 1769476
  85.3 0.9 copy-start.2

commit v3 on v2

--- a/solution.py
+++ b/solution.py
@@ -186,43 +186,37 @@
 
 
 def others_kernel(me_ref, *refs):
-    h_refs = refs[: len(refs) - 3]
-    up_ref, slope_ref, act_ref = refs[len(refs) - 3 :]
-    for g, h_ref in enumerate(h_refs):
+    h_refs = refs[: len(refs) - 4]
+    up_ref, slope_ref, act_ref, hsel_ref = refs[len(refs) - 4 :]
+    width = h_refs[0].shape[1]
+    out_rows = hsel_ref.shape[1]
+
+    @pl.when(pl.program_id(0) == 0)
+    def _():
+        row = lax.broadcasted_iota(jnp.int32, (out_rows, width), 0) + me_ref[0] * out_rows
+        pick = (row == lax.broadcasted_iota(jnp.int32, (out_rows, width), 1)).astype(jnp.bfloat16)
+        for g, h_ref in enumerate(h_refs):
+            hsel_ref[g] = contract_cols(pick, h_ref[...]).astype(jnp.bfloat16)
+
+    for g, h_ref in enumerate(h_refs[1:]):
         pre = jnp.dot(h_ref[...], up_ref[...], preferred_element_type=jnp.float32)
         value, slope = gelu_parts(pre)
         slope_ref[g] = slope.astype(jnp.bfloat16)
         act_ref[g] = value.astype(jnp.bfloat16)
 
 
-def up_kernel(groups, me_ref, *refs):
-    mid_refs = refs[: groups - 1]
-    h_refs = refs[groups - 1 : 2 * groups - 1]
-    down_ref, slope_ref, own_ref, up_ref, hsel = refs[2 * groups - 1 :]
-    width = h_refs[0].shape[1]
-    out_rows = up_ref.shape[0]
-
-    @pl.when(pl.program_id(0) == 0)
-    def _():
-        row = lax.broadcasted_iota(jnp.int32, (out_rows, width), 0) + me_ref[0] * out_rows
-        pick = (row == lax.broadcasted_iota(jnp.int32, (out_rows, width), 1)).astype(jnp.bfloat16)
-        for g, h_ref in enumerate(h_refs):
-            hsel[g] = contract_cols(pick, h_ref[...]).astype(jnp.bfloat16)
-
-    total = jnp.dot(hsel[0], own_ref[...], preferred_element_type=jnp.float32)
+def weights_kernel(groups, me_ref, *refs):
+    mid_refs = refs[:groups]
+    hsel_ref, down_ref, slope_ref, own_ref, act_own_ref, act_ref, up_ref, out_ref = refs[groups:]
+    total = jnp.dot(hsel_ref[0], own_ref[...], preferred_element_type=jnp.float32)
+    rows = dot_rows(act_own_ref[...], mid_refs[0][...])
     for g in range(groups - 1):
-        grad_act = contract_cols(mid_refs[g][...], down_ref[...])
+        grad_act = contract_cols(mid_refs[g + 1][...], down_ref[...])
         grad_pre = (grad_act * slope_ref[g].astype(jnp.float32)).astype(jnp.bfloat16)
-        total += jnp.dot(hsel[g + 1], grad_pre, preferred_element_type=jnp.float32)
+        total += jnp.dot(hsel_ref[g + 1], grad_pre, preferred_element_type=jnp.float32)
+        rows += dot_rows(act_ref[g], mid_refs[g + 1][...])
     up_ref[...] = total
-
-
-def down_kernel(me_ref, own_ref, act_ref, *refs):
-    mid_refs, out_ref = refs[:-1], refs[-1]
-    total = dot_rows(own_ref[...], mid_refs[0][...])
-    for g in range(len(mid_refs) - 1):
-        total += dot_rows(act_ref[g], mid_refs[g + 1][...])
-    out_ref[...] = total
+    out_ref[...] = rows
 
 
 def params():
@@ -312,67 +306,59 @@
     tile_a = own_cols
     own_tiles = own_cols // tile_a
     steps_a = hidden // tile_a
-    o_slope, o_act = pl.pallas_call(
+    out_rows = width // groups
+    o_slope, o_act, hsel = pl.pallas_call(
         others_kernel,
         grid_spec=pltpu.PrefetchScalarGridSpec(
             num_scalar_prefetch=1,
             grid=(steps_a,),
-            in_specs=[whole(rows, width)] * (groups - 1)
+            in_specs=[whole(rows, width)] * groups
             + [pl.BlockSpec((width, tile_a), lambda f, m: (0, lax.rem(f + (m[0] + 1) * own_tiles, steps_a)))],
             out_specs=[
                 pl.BlockSpec((groups - 1, rows, tile_a), lambda f, m: (0, 0, lax.rem(f + (m[0] + 1) * own_tiles, steps_a))),
                 pl.BlockSpec((groups - 1, rows, tile_a), lambda f, m: (0, 0, jnp.maximum(f + own_tiles - steps_a, 0))),
+                whole(groups, out_rows, rows),
             ],
         ),
         out_shape=[
             jax.ShapeDtypeStruct((groups - 1, rows, hidden), bf),
             jax.ShapeDtypeStruct((groups - 1, rows, own_cols), bf),
+            jax.ShapeDtypeStruct((groups, out_rows, rows), bf),
         ],
         compiler_params=params(),
         cost_estimate=cost((groups - 1) * unit, 3 * wbytes),
         name="others",
-    )(me_arr, *others_h, up_mat)
-
-    out_rows = width // groups
-    grad_up = pl.pallas_call(
-        functools.partial(up_kernel, groups),
+    )(me_arr, hidden_in, *others_h, up_mat)
+
+    parts = hidden // TILE_U
+    part = own_cols // parts
+    grad_up, grad_down = pl.pallas_call(
+        functools.partial(weights_kernel, groups),
         grid_spec=pltpu.PrefetchScalarGridSpec(
             num_scalar_prefetch=1,
-            grid=(hidden // TILE_U,),
-            in_specs=[whole(rows, width)] * (2 * groups - 1)
+            grid=(parts,),
+            in_specs=[whole(rows, width)] * groups
             + [
+                whole(groups, out_rows, rows),
                 pl.BlockSpec((TILE_U, width), lambda f, m: (f, 0)),
                 pl.BlockSpec((groups - 1, rows, TILE_U), lambda f, m: (0, 0, f)),
                 pl.BlockSpec((rows, TILE_U), lambda f, m: (0, f)),
-            ],
-            out_specs=pl.BlockSpec((out_rows, TILE_U), lambda f, m: (0, f)),
-            scratch_shapes=[pltpu.VMEM((groups, out_rows, rows), bf)],
-        ),
-        out_shape=jax.ShapeDtypeStruct((out_rows, hidden), f32),
-        compiler_params=params(),
-        cost_estimate=cost(groups * unit, 5 * wbytes),
-        name="upgrad",
-    )(me_arr, *others_mid, hidden_in, *others_h, down_mat, o_slope, grad_pre)
-
-    part = own_cols // 3 if own_cols % 384 == 0 else own_cols
-    parts = own_cols // part
-    grad_down = pl.pallas_call(
-        down_kernel,
-        grid_spec=pltpu.PrefetchScalarGridSpec(
-            num_scalar_prefetch=1,
-            grid=(parts,),
-            in_specs=[
                 pl.BlockSpec((rows, part), lambda f, m: (0, f + m[0] * parts)),
                 pl.BlockSpec((groups - 1, rows, part), lambda f, m: (0, 0, f)),
-            ]
-            + [whole(rows, width)] * groups,
-            out_specs=pl.BlockSpec((part, width), lambda f, m: (f, 0)),
+            ],
+            out_specs=[
+                pl.BlockSpec((out_rows, TILE_U), lambda f, m: (0, f)),
+                pl.BlockSpec((part, width), lambda f, m: (f, 0)),
+            ],
         ),
-        out_shape=jax.ShapeDtypeStruct((own_cols, width), f32),
-        compiler_params=params(),
-        cost_estimate=cost(unit, 2 * wbytes),
-        name="downgrad",
-    )(me_arr, active, o_act, mid, *others_mid)
+        out_shape=[
+            jax.ShapeDtypeStruct((out_rows, hidden), f32),
+            jax.ShapeDtypeStruct((own_cols, width), f32),
+        ],
+        compiler_params=params(),
+        cost_estimate=cost((groups + 1) * unit, 6 * wbytes),
+        name="weights",
+    )(me_arr, mid, *others_mid, hsel, down_mat, o_slope, grad_pre, active, o_act)
 
     embed_t = (sum_t.astype(f32) + swapped.astype(f32)).astype(bf)
     target = owner_dev[0, :, 0] * HOT + slot_row[0]
@@ -394,7 +380,7 @@
         P("token", "dp", None),
         P("token", "dp"),
     )
-    small = mesh.shape["dp"] <= 4
+    small = mesh.shape["dp"] == 4
 
     def layer(*args):
         return (small_group if small else per_device)(*args)

time: 109 us -> 113 us (1.037)
  waiting for transfers between devices: 27.7 us -> 34.2 us
  Pallas kernels: 56.9 us -> 54.1 us
    ppermute x6, waiting for transfers between devices: 27.7 us -> 34.1 us  [gather_groups(): taken.append(lax.ppermute(value, 'dp', [(i, i ^ k) for i in range(groups)]))]
    pallas_call x2 -> x1, Pallas kernels: 21.2 us -> 17.3 us  [small_group(): pl.pallas_call(functools.partial(weights_kernel, groups), grid_spec=pltpu...]
    pallas_call x1, Pallas kernels: 12.7 us -> 14 us  [small_group(): pl.pallas_call(others_kernel, grid_spec=pltpu.PrefetchScalarGridSpec(num_...]
  transfers between devices with their start and end apart: 8 -> 8, of which waited for: 4 -> 3; matrix products, arithmetic and copies ran while one was open for 3% -> 3% of each run, Pallas kernels for 31% -> 28%
where the time goes in v3:
time: 113 us; the launch traced here: 112 us
  Pallas kernels  54.1 us (48%)
  waiting for transfers between devices  34.2 us (30%)
  starting transfers between devices  19.1 us (17%)
  matrix products  3.27 us (3%)
    ppermute x6, waiting for transfers between devices, gather_groups(): taken.append(lax.ppermute(value, 'dp', [(i, i ^ k) for i in range(groups)]))  34.1 us
    pallas_call x1, Pallas kernels, small_group(): pl.pallas_call(functools.partial(weights_kernel, groups), grid_spec=pltpu...  17.3 us
    pallas_call x1, Pallas kernels, small_group(): pl.pallas_call(others_kernel, grid_spec=pltpu.PrefetchScalarGridSpec(num_...  14 us
    pallas_call x1, Pallas kernels, small_group(): pl.pallas_call(backward_kernel, grid=(steps,), in_specs=[whole(rows, widt...  10.6 us
    pallas_call x1, Pallas kernels, small_group(): pl.pallas_call(forward_kernel, grid=(steps,), in_specs=[whole(rows, width...  9.95 us
    ppermute x6, starting transfers between devices, gather_groups(): taken.append(lax.ppermute(value, 'dp', [(i, i ^ k) for i in range(groups)]))  9 us
    all_to_all x1, starting transfers between devices, small_group(): lax.all_to_all(sum_t.reshape(pieces, width // pieces, rows), 'token', spl...  6.36 us
    all_to_all x1, starting transfers between devices, small_group(): lax.all_to_all(partial_rows, 'dp', split_axis=0, concat_axis=0, tiled=True)  3.74 us
  transfers between devices with their start and end apart: 8, of which 3 were waited for; matrix products, arithmetic and copies ran while one was open for 3% of the time, Pallas kernels for 28%

profile of v3, /device:TPU:0, one launch (start us, length us, event | category | flops | bytes accessed | tf_op | source)
XLA Modules:
  0.0 112.5 jit_solution(14277163108657533585)
XLA Ops:
  0.6 2.3 %norm.1.h_ref.refs_0_ = bf16[384,768]{1,0:T(8,128)(2,1)} custom-call(bf16[384,768]{1,0:T(8,128)(2,1)} %bitcast.22, f32[1,768]{1,0:T(1,128)} %gain_ref.5), custom_call_target="tpu_custom_call" | custom-call | tf_op jit(solution)/shard_map/norm/pallas_call | solution.py:252
  2.9 9.9 %forward.1 = (bf16[384,3072]{1,0:T(8,128)(2,1)}, bf16[384,3072]{1,0:T(8,128)(2,1)}, f32[384,768]{1,0:T(8,128)}, bf16[384,768]{1,0:T(8,128)(2,1)}) custom-call(bf16[384,768]{1,0:T(8,128)(2,1)} %norm.1.h_ref.refs_0_, bf16[768,3072]{1,0:T(8,128)(2,1)} %bitcast.16, bf16[3072,768]{1,0:T(8,128)(2,1)} %bitcast.19, bf16[384,768]{1,0:T(8,128)(2,1)} %bitcast.27, ...), custom_call_target="tpu_custom_call" | custom-call | flops 3623878656 | bytes 14155776 | tf_op jit(solution)/shard_map/forward/pallas_call | solution.py:266
  12.8 0.0 copy-start
  12.9 0.0 copy-start.1
  12.9 0.0 copy-start.2
  12.9 0.0 copy-start.3
  12.9 10.6 %backward.1 = (bf16[384,3072]{1,0:T(8,128)(2,1)}, bf16[768,384]{1,0:T(8,128)(2,1)}) custom-call(bf16[384,768]{1,0:T(8,128)(2,1)} %get-tuple-element.14.mid_ref.refs_0_, bf16[3072,768]{1,0:T(8,128)(2,1)} %bitcast.20, bf16[768,3072]{1,0:T(8,128)(2,1)} %bitcast.17, bf16[384,3072]{1,0:T(8,128)(2,1)} %get-tuple-element.17.slope_ref, ...), custom_call_target="tpu_custom_call" | custom-call | flops 3623878656 | bytes 14155776 | tf_op jit(solution)/shard_map/backward/pallas_call | solution.py:283
  23.5 6.4 %all-to-all-start = ((bf16[8,96,384]{2,1,0:T(8,128)(2,1)}), bf16[8,96,384]{2,1,0:T(8,128)(2,1)S(1)}, u32[]{:S(2)}, u32[]{:S(2)}) async-start(bf16[8,96,384]{2,1,0:T(8,128)(2,1)} %bitcast.25), calls=%async_computation | async-start | bytes 1179648 | tf_op jit(solution)/shard_map/all_to_all | solution.py:301
  29.9 0.0 copy-done
  29.9 1.6 %collective-permute-start.3 = (bf16[384,768]{1,0:T(8,128)(2,1)S(1)}, bf16[384,768]{1,0:T(8,128)(2,1)S(1)}, u32[]{:S(2)}, u32[]{:S(2)}) collective-permute-start(bf16[384,768]{1,0:T(8,128)(2,1)S(1)} %copy-done), channel_id=1, source_target_pairs={{0,8},{8,0},{16,24},{24,16},{1,9},{9,1},{17,25},{25,17},{2,10},{10... | collective-permute-start | bytes 1769480 | tf_op jit(solution)/shard_map/ppermute | solution.py:237
  31.4 1.5 %collective-permute-start.4 = (bf16[384,768]{1,0:T(8,128)(2,1)S(1)}, bf16[384,768]{1,0:T(8,128)(2,1)}, u32[]{:S(2)}, u32[]{:S(2)}) collective-permute-start(bf16[384,768]{1,0:T(8,128)(2,1)S(1)} %copy-done), channel_id=1, source_target_pairs={{0,16},{8,24},{16,0},{24,8},{1,17},{9,25},{17,1},{25,9},{2,18},{10... | collective-permute-start | bytes 1769480 | tf_op jit(solution)/shard_map/ppermute | solution.py:237
  33.0 0.5 collective-permute-start.5
  33.4 0.0 copy-done.1
  33.5 1.5 %collective-permute-start = (bf16[384,768]{1,0:T(8,128)(2,1)S(1)}, bf16[384,768]{1,0:T(8,128)(2,1)S(1)}, u32[]{:S(2)}, u32[]{:S(2)}) collective-permute-start(bf16[384,768]{1,0:T(8,128)(2,1)S(1)} %copy-done.1), channel_id=1, source_target_pairs={{0,8},{8,0},{16,24},{24,16},{1,9},{9,1},{17,25},{25,17},{2,10},{10... | collective-permute-start | bytes 1769480 | tf_op jit(solution)/shard_map/ppermute | solution.py:237
  34.9 1.5 %collective-permute-start.1 = (bf16[384,768]{1,0:T(8,128)(2,1)S(1)}, bf16[384,768]{1,0:T(8,128)(2,1)}, u32[]{:S(2)}, u32[]{:S(2)}) collective-permute-start(bf16[384,768]{1,0:T(8,128)(2,1)S(1)} %copy-done.1), channel_id=1, source_target_pairs={{0,16},{8,24},{16,0},{24,8},{1,17},{9,25},{17,1},{25,9},{2,18},{10... | collective-permute-start | bytes 1769480 | tf_op jit(solution)/shard_map/ppermute | solution.py:237
  36.5 0.0 copy-done.2
  36.5 0.0 copy-done.3
  36.5 9.7 %collective-permute-done.3.refs_1_ = bf16[384,768]{1,0:T(8,128)(2,1)S(1)} collective-permute-done((bf16[384,768]{1,0:T(8,128)(2,1)S(1)}, bf16[384,768]{1,0:T(8,128)(2,1)S(1)}, u32[]{:S(2)}, u32[]{:S(2)}) %collective-permute-start.3) | collective-permute-done | bytes 589856 | tf_op jit(solution)/shard_map/ppermute | solution.py:237
  46.2 0.0 copy-start.5
  46.2 2.4 %collective-permute-start.2 = (bf16[384,768]{1,0:T(8,128)(2,1)S(1)}, bf16[384,768]{1,0:T(8,128)(2,1)}, u32[]{:S(2)}, u32[]{:S(2)}) collective-permute-start(bf16[384,768]{1,0:T(8,128)(2,1)S(1)} %copy-done.1), channel_id=1, source_target_pairs={{0,24},{8,16},{16,8},{24,0},{1,25},{9,17},{17,9},{25,1},{2,26},{10... | collective-permute-start | bytes 1769480 | tf_op jit(solution)/shard_map/ppermute | solution.py:237
  48.6 0.0 all-to-all-done
  48.6 3.3 %convolution_convert_fusion = bf16[1024,768]{1,0:T(8,128)(2,1)} fusion(s32[384]{0:T(512)S(1)} %fusion.3, bf16[768,384]{1,0:T(8,128)(2,1)S(1)} %bitcast.26, bf16[768,384]{1,0:T(8,128)(2,1)} %get-tuple-element.24), kind=kOutput, calls=%fused_computation.1 | convolution fusion | flops 606339072 | bytes 2754048 | tf_op jit(solution)/shard_map/dot_general | solution.py:44
  51.9 0.0 copy-done.5
  51.9 3.7 %all-to-all-start.1 = ((bf16[4,256,768]{2,1,0:T(8,128)(2,1)}), bf16[4,256,768]{2,1,0:T(8,128)(2,1)S(1)}, u32[]{:S(2)}, u32[]{:S(2)}) async-start(bf16[4,256,768]{2,1,0:T(8,128)(2,1)} %bitcast.10), calls=%async_computation.1 | async-start | bytes 3145728 | tf_op jit(solution)/shard_map/all_to_all | solution.py:367
  55.6 4.8 %collective-permute-done.4.refs_2_ = bf16[384,768]{1,0:T(8,128)(2,1)} collective-permute-done((bf16[384,768]{1,0:T(8,128)(2,1)S(1)}, bf16[384,768]{1,0:T(8,128)(2,1)}, u32[]{:S(2)}, u32[]{:S(2)}) %collective-permute-start.4) | collective-permute-done | bytes 589856 | tf_op jit(solution)/shard_map/ppermute | solution.py:237
  60.4 0.0 collective-permute-done.5.refs_3_
  60.4 14.0 %others.1 = (bf16[3,384,3072]{2,1,0:T(8,128)(2,1)}, bf16[3,384,768]{2,1,0:T(8,128)(2,1)}, bf16[4,192,384]{2,1,0:T(8,128)(2,1)}) custom-call(s32[1]{0:T(128)} %bitcast.me_ref, bf16[384,768]{1,0:T(8,128)(2,1)} %norm.1.h_ref.refs_0_, bf16[384,768]{1,0:T(8,128)(2,1)} %copy-done.5, bf16[384,768]{1,0:T(8,128)(2,1)} %collective-permute-done.4.refs_2_, ...), custom_call_target="tpu_custom_call" | custom-call | flops 5435817984 | bytes 14155776 | tf_op jit(solution)/shard_map/others/pallas_call | solution.py:310
  74.4 0.0 collective-permute-done.refs_1_
  74.4 0.0 copy-start.4
  74.4 19.7 %collective-permute-done.1.refs_2_ = bf16[384,768]{1,0:T(8,128)(2,1)} collective-permute-done((bf16[384,768]{1,0:T(8,128)(2,1)S(1)}, bf16[384,768]{1,0:T(8,128)(2,1)}, u32[]{:S(2)}, u32[]{:S(2)}) %collective-permute-start.1) | collective-permute-done | bytes 589856 | tf_op jit(solution)/shard_map/ppermute | solution.py:237
  94.1 0.0 collective-permute-done.2.refs_3_
  94.1 0.0 copy-done.4
  94.1 17.3 %weights.1 = (f32[192,3072]{1,0:T(8,128)}, f32[768,768]{1,0:T(8,128)}) custom-call(s32[1]{0:T(128)} %bitcast.me_ref, bf16[384,768]{1,0:T(8,128)(2,1)} %get-tuple-element.14.mid_ref.refs_0_, bf16[384,768]{1,0:T(8,128)(2,1)} %copy-done.4, bf16[384,768]{1,0:T(8,128)(2,1)} %collective-permute-done.1.refs_2_, bf16[384,768]{1,0:T(8,128)(2,1)} %collective-permute-done.2.refs_3_, ...), custom_call_target="tpu_custom_call" | custom-call | flops 9059696640 | bytes 28311552 | tf_op jit(solution)/shard_map/weights/pallas_call | solution.py:335
  111.4 0.0 all-to-all-done.1
  111.4 1.1 convert_reduce_fusion
  (1 shorter events, 0.0 us)
Async XLA Ops:
  12.8 17.0 %copy-start = (bf16[384,768]{1,0:T(8,128)(2,1)S(1)}, bf16[384,768]{1,0:T(8,128)(2,1)}, u32[]{:S(2)}) copy-start(bf16[384,768]{1,0:T(8,128)(2,1)} %norm.1.h_ref.refs_0_) | copy-start | bytes 1769476
  12.9 20.6 %copy-start.1 = (bf16[384,768]{1,0:T(8,128)(2,1)S(1)}, bf16[384,768]{1,0:T(8,128)(2,1)}, u32[]{:S(2)}) copy-start(bf16[384,768]{1,0:T(8,128)(2,1)} %get-tuple-element.14.mid_ref.refs_0_) | copy-start | bytes 1769476
  12.9 23.6 %copy-start.2 = (s32[1,384]{1,0:T(1,128)S(1)}, s32[1,384]{1,0:T(1,128)}, u32[]{:S(2)}) copy-start(s32[1,384]{1,0:T(1,128)} %param.15) | copy-start | bytes 4612
  12.9 23.6 %copy-start.3 = (s32[1,384,1]{1,2,0:T(1,128)S(1)}, s32[1,384,1]{1,2,0:T(1,128)}, u32[]{:S(2)}) copy-start(s32[1,384,1]{1,2,0:T(1,128)} %param.14) | copy-start | bytes 4612
  23.5 25.1 %all-to-all-start = ((bf16[8,96,384]{2,1,0:T(8,128)(2,1)}), bf16[8,96,384]{2,1,0:T(8,128)(2,1)S(1)}, u32[]{:S(2)}, u32[]{:S(2)}) async-start(bf16[8,96,384]{2,1,0:T(8,128)(2,1)} %bitcast.25), calls=%async_computation | async-start | bytes 1179648 | tf_op jit(solution)/shard_map/all_to_all | solution.py:301
  29.9 16.3 %collective-permute-start.3 = (bf16[384,768]{1,0:T(8,128)(2,1)S(1)}, bf16[384,768]{1,0:T(8,128)(2,1)S(1)}, u32[]{:S(2)}, u32[]{:S(2)}) collective-permute-start(bf16[384,768]{1,0:T(8,128)(2,1)S(1)} %copy-done), channel_id=1, source_target_pairs={{0,8},{8,0},{16,24},{24,16},{1,9},{9,1},{17,25},{25,17},{2,10},{10... | collective-permute-start | bytes 1769480 | tf_op jit(solution)/shard_map/ppermute | solution.py:237
  31.4 28.9 %collective-permute-start.4 = (bf16[384,768]{1,0:T(8,128)(2,1)S(1)}, bf16[384,768]{1,0:T(8,128)(2,1)}, u32[]{:S(2)}, u32[]{:S(2)}) collective-permute-start(bf16[384,768]{1,0:T(8,128)(2,1)S(1)} %copy-done), channel_id=1, source_target_pairs={{0,16},{8,24},{16,0},{24,8},{1,17},{9,25},{17,1},{25,9},{2,18},{10... | collective-permute-start | bytes 1769480 | tf_op jit(solution)/shard_map/ppermute | solution.py:237
  33.0 27.4 %collective-permute-start.5 = (bf16[384,768]{1,0:T(8,128)(2,1)S(1)}, bf16[384,768]{1,0:T(8,128)(2,1)}, u32[]{:S(2)}, u32[]{:S(2)}) collective-permute-start(bf16[384,768]{1,0:T(8,128)(2,1)S(1)} %copy-done), channel_id=1, source_target_pairs={{0,24},{8,16},{16,8},{24,0},{1,25},{9,17},{17,9},{25,1},{2,26},{10... | collective-permute-start | bytes 1769480 | tf_op jit(solution)/shard_map/ppermute | solution.py:237
  33.5 40.9 %collective-permute-start = (bf16[384,768]{1,0:T(8,128)(2,1)S(1)}, bf16[384,768]{1,0:T(8,128)(2,1)S(1)}, u32[]{:S(2)}, u32[]{:S(2)}) collective-permute-start(bf16[384,768]{1,0:T(8,128)(2,1)S(1)} %copy-done.1), channel_id=1, source_target_pairs={{0,8},{8,0},{16,24},{24,16},{1,9},{9,1},{17,25},{25,17},{2,10},{10... | collective-permute-start | bytes 1769480 | tf_op jit(solution)/shard_map/ppermute | solution.py:237
  34.9 59.2 %collective-permute-start.1 = (bf16[384,768]{1,0:T(8,128)(2,1)S(1)}, bf16[384,768]{1,0:T(8,128)(2,1)}, u32[]{:S(2)}, u32[]{:S(2)}) collective-permute-start(bf16[384,768]{1,0:T(8,128)(2,1)S(1)} %copy-done.1), channel_id=1, source_target_pairs={{0,16},{8,24},{16,0},{24,8},{1,17},{9,25},{17,1},{25,9},{2,18},{10... | collective-permute-start | bytes 1769480 | tf_op jit(solution)/shard_map/ppermute | solution.py:237
  46.2 5.7 %copy-start.5 = (bf16[384,768]{1,0:T(8,128)(2,1)}, bf16[384,768]{1,0:T(8,128)(2,1)S(1)}, u32[]{:S(2)}) copy-start(bf16[384,768]{1,0:T(8,128)(2,1)S(1)} %collective-permute-done.3.refs_1_) | copy-start | bytes 1769476
  46.2 47.9 %collective-permute-start.2 = (bf16[384,768]{1,0:T(8,128)(2,1)S(1)}, bf16[384,768]{1,0:T(8,128)(2,1)}, u32[]{:S(2)}, u32[]{:S(2)}) collective-permute-start(bf16[384,768]{1,0:T(8,128)(2,1)S(1)} %copy-done.1), channel_id=1, source_target_pairs={{0,24},{8,16},{16,8},{24,0},{1,25},{9,17},{17,9},{25,1},{2,26},{10... | collective-permute-start | bytes 1769480 | tf_op jit(solution)/shard_map/ppermute | solution.py:237
  51.9 59.5 %all-to-all-start.1 = ((bf16[4,256,768]{2,1,0:T(8,128)(2,1)}), bf16[4,256,768]{2,1,0:T(8,128)(2,1)S(1)}, u32[]{:S(2)}, u32[]{:S(2)}) async-start(bf16[4,256,768]{2,1,0:T(8,128)(2,1)} %bitcast.10), calls=%async_computation.1 | async-start | bytes 3145728 | tf_op jit(solution)/shard_map/all_to_all | solution.py:367
  74.4 19.7 %copy-start.4 = (bf16[384,768]{1,0:T(8,128)(2,1)}, bf16[384,768]{1,0:T(8,128)(2,1)S(1)}, u32[]{:S(2)}) copy-start(bf16[384,768]{1,0:T(8,128)(2,1)S(1)} %collective-permute-done.refs_1_) | copy-start | bytes 1769476
